TPU v7x, 128 devices: a whole 4x4x4 slice. The times are simulated.
128 devices in a mesh: dp: 32 (over x, z, y_hi), crop: 4 (over y_lo, core).
Axes of the slice: x: 4, y: 4 (y_hi: 2, y_lo: 2; y = y_hi * 2 + y_lo), z: 4, core: 2. Of those that a mesh axis runs over, the one named last changes fastest.
Arguments:
- query_crops: bfloat16 [65536, 2048], P(('dp', 'crop')), may hold values from -6 to 6
- key_crops: bfloat16 [65536, 2048], P(('dp', 'crop')), may hold values from -43 to 43
- shuffle: int32 [65536], P(('dp', 'crop')), may hold values from 0 to 65535, as said below
- distractor_bank: bfloat16 [16384, 128], replicated, may hold values from -2.5 to 2.5
- query_inner: bfloat16 [2048, 2048], replicated, may hold values from -0.125 to 0.125
- query_outer: bfloat16 [2048, 128], replicated, may hold values from -0.125 to 0.125
- key_inner: bfloat16 [2048, 2048], replicated, may hold values from -0.125 to 0.125
- key_outer: bfloat16 [2048, 128], replicated, may hold values from -0.125 to 0.125
Outputs:
- grad_inner: float32 [2048, 2048], P(('dp', 'crop'))
- grad_outer: float32 [2048, 128], P(('dp', 'crop'))
Inputs may be any that keep to these rules, and one draw needn't show every extreme that they name: `shuffle`: a permutation of the 65536 key crops; shuffled position t * 512 + s * 4 + j, for j below 4, takes a crop from rows s * 512 up to (s + 1) * 512 - 1.
All inputs are finite; a program needn't handle non-finite values.
Results may differ from a plain program's by a relative error of at most 0.008.
Values may be sent and summed in bfloat16 or wider, within the bound.
A program may use at most 192 MiB of HBM per device.

v0:
```python
import jax
import jax.numpy as jnp
from jax import lax
from jax.sharding import PartitionSpec as P

sharpness_divisor = 0.2
loss_scale = 4096.0
bn_eps = 1e-05
norm_eps = 1e-06


def batch_stats(hidden):
    average = jnp.mean(hidden, axis=0)
    variance = jnp.mean(hidden * hidden, axis=0) - average * average
    return (average, lax.rsqrt(variance + bn_eps))


def head_tail(normed, w_out):
    active = jnp.maximum(normed, 0.0).astype(jnp.bfloat16)
    projected = jnp.dot(active, w_out, preferred_element_type=jnp.float32)
    return projected * lax.rsqrt(jnp.sum(projected * projected, axis=-1, keepdims=True) + norm_eps)


def key_embed(crop_rows, w_in, w_out):
    hidden = jnp.dot(crop_rows, w_in, preferred_element_type=jnp.float32)
    average, inv_std = batch_stats(hidden)
    return head_tail((hidden - average) * inv_std, w_out)


def query_grads(crop_rows, matching_targets, distractor_bank, w_in, w_out, all_rows):
    hidden = jnp.dot(crop_rows, w_in, preferred_element_type=jnp.float32)
    average, inv_std = batch_stats(hidden)
    normed = (hidden - average) * inv_std
    active = jnp.maximum(normed, 0.0).astype(jnp.bfloat16)
    projected = jnp.dot(active, w_out, preferred_element_type=jnp.float32)
    inv_len = lax.rsqrt(jnp.sum(projected * projected, axis=-1, keepdims=True) + norm_eps)
    probe_features = projected * inv_len
    matching_similarity = (
        jnp.sum(probe_features * matching_targets, axis=-1, keepdims=True) / sharpness_divisor
    )
    distractor_similarities = (
        lax.dot_general(
            probe_features.astype(jnp.bfloat16),
            distractor_bank,
            (((1,), (1,)), ((), ())),
            preferred_element_type=jnp.float32,
        )
        / sharpness_divisor
    )
    exp_pos = jnp.exp(matching_similarity)
    exp_neg = jnp.exp(distractor_similarities)
    total_exp = exp_pos + jnp.sum(exp_neg, axis=-1, keepdims=True)
    scale_coef = loss_scale / all_rows
    matching_similarity_slope = scale_coef * (exp_pos / total_exp - 1.0)
    distractor_similarity_slope = (scale_coef * exp_neg / total_exp).astype(jnp.bfloat16)
    probe_feature_slope = (
        matching_similarity_slope * matching_targets
        + jnp.dot(distractor_similarity_slope, distractor_bank, preferred_element_type=jnp.float32)
    ) / sharpness_divisor
    d_proj = (
        (
            probe_feature_slope
            - probe_features * jnp.sum(probe_feature_slope * probe_features, axis=-1, keepdims=True)
        )
        * inv_len
    ).astype(jnp.bfloat16)
    grad_out = lax.dot_general(
        active, d_proj, (((0,), (0,)), ((), ())), preferred_element_type=jnp.float32
    )
    d_act = lax.dot_general(
        d_proj, w_out, (((1,), (1,)), ((), ())), preferred_element_type=jnp.float32
    )
    d_norm = jnp.where(normed > 0.0, d_act, 0.0)
    d_hidden = inv_std * (
        d_norm - jnp.mean(d_norm, axis=0) - normed * jnp.mean(d_norm * normed, axis=0)
    )
    grad_in = lax.dot_general(
        crop_rows,
        d_hidden.astype(jnp.bfloat16),
        (((0,), (0,)), ((), ())),
        preferred_element_type=jnp.float32,
    )
    return (grad_in, grad_out)


def per_device(
    query_crops, key_crops, shuffle, distractor_bank, query_inner, query_outer, key_inner, key_outer
):
    group_count = lax.axis_size(("dp", "crop"))
    row_count = query_crops.shape[0]
    per_peer = row_count // group_count
    all_rows = float(row_count * group_count)
    wanted = (shuffle % row_count).reshape(group_count, per_peer)
    requested = lax.all_to_all(wanted, ("dp", "crop"), split_axis=0, concat_axis=0, tiled=True)
    flat_req = requested.reshape(-1)
    outgoing = key_crops[flat_req].reshape(group_count, per_peer, key_crops.shape[1])
    incoming = lax.all_to_all(
        outgoing, ("dp", "crop"), split_axis=0, concat_axis=0, tiled=True
    ).reshape(row_count, key_crops.shape[1])
    embedded = key_embed(incoming, key_inner, key_outer).reshape(
        group_count, per_peer, key_outer.shape[1]
    )
    returned = lax.all_to_all(
        embedded, ("dp", "crop"), split_axis=0, concat_axis=0, tiled=True
    ).reshape(row_count, key_outer.shape[1])
    matching_targets = (
        jnp.zeros((row_count, returned.shape[1]), jnp.float32).at[flat_req].set(returned)
    )
    grad_in, grad_out = query_grads(
        query_crops, matching_targets, distractor_bank, query_inner, query_outer, all_rows
    )
    grad_in, grad_out = (
        lax.psum_scatter(grad_in, ("dp", "crop"), scatter_dimension=0, tiled=True),
        lax.psum_scatter(grad_out, ("dp", "crop"), scatter_dimension=0, tiled=True),
    )
    return (grad_in, grad_out)


def solution(mesh):
    placed = (
        P(("dp", "crop"), None),
        P(("dp", "crop"), None),
        P(("dp", "crop")),
        P(),
        P(),
        P(),
        P(),
        P(),
    )
    return jax.shard_map(
        per_device,
        mesh=mesh,
        in_specs=placed,
        out_specs=(P(("dp", "crop"), None), P(("dp", "crop"), None)),
        check_vma=False,
    )
```

profile of v0, /device:TPU:0, one launch (start us, length us, event | category | flops | bytes accessed | tf_op | source)
XLA Modules:
  0.0 1461.1 jit_solution(13961770459133875253)
XLA Ops:
  7.2 0.0 copy-start
  7.2 0.8 add_select_fusion
  8.0 0.1 all_to_all.12
  8.1 20.3 %all_to_all.19 = s32[128,1,4]{2,1,0:T(1,128)S(1)} all-to-all(s32[128,1,4]{2,1,0:T(1,128)S(1)} %bitcast.21), channel_id=1, replica_groups=mesh['dp'=32,'crop'=4] {'dp','crop'}, dimensions={0} | all-to-all | bytes 4096 | tf_op jit(solution)/shard_map/all_to_all | solution.py:94
  28.4 0.5 broadcast.154
  29.0 0.8 reduce.3
  29.8 0.1 reshape.115
  29.9 7.2 gather_fusion
  37.1 4.1 reshape.116
  41.2 5.8 all-to-all-start.1
  47.0 0.0 copy-done
  47.0 0.0 copy-start.2
  47.0 7.0 multiply_reduce_fusion.2
  54.0 0.0 copy-start.1
  54.0 2.0 copy-done.1
  56.0 0.0 copy-done.2
  56.0 0.8 multiply_reduce_fusion.6
  56.9 20.0 %all-to-all-done.1 = bf16[128,4,2048]{2,1,0:T(4,128)(2,1)} async-done(((bf16[128,4,2048]{2,1,0:T(4,128)(2,1)}), bf16[128,4,2048]{2,1,0:T(4,128)(2,1)}, u32[]{:S(2)}, u32[]{:S(2)}) %all-to-all-start.1) | async-done | bytes 2097184 | tf_op jit(solution)/shard_map/all_to_all | solution.py:97
  76.9 4.0 reshape.117
  80.9 0.0 copy-start.3
  80.9 7.7 fusion.26
  88.6 0.0 copy-done.3
  88.6 0.8 multiply_reduce_fusion.5
  89.4 0.9 broadcast_multiply_fusion
  90.2 4.6 all-to-all-start.2
  94.8 0.2 reduce-scatter.5.cloned.1.call-start
  95.0 15.6 %fusion = (f32[512]{0:T(512)S(1)}, f32[512,16384]{1,0:T(8,128)}) fusion(bf16[16384,128]{1,0:T(8,128)(2,1)} %param.11, f32[512,128]{0,1:T(8,128)S(1)} %get-tuple-element.22, f32[512]{0:T(512)S(1)} %add_rsqrt_fusion.3), kind=kOutput, calls=%fused_computation.4 | convolution fusion | flops 2164391424 | bytes 38014976 | tf_op jit(solution)/shard_map/dot_general | solution.py:42
  110.6 0.0 all-to-all-done.2
  110.6 1.8 scatter_custom_fusion
  112.4 0.1 copy.16
  112.5 0.1 multiply_reduce_fusion.4
  112.6 15.9 %multiply_reduce_fusion.3 = (f32[512]{0:T(512)S(1)}, f32[512,128]{0,1:T(8,128)S(1)}) fusion(f32[512,128]{0,1:T(8,128)S(1)} %get-tuple-element.22, f32[512]{0:T(512)S(1)} %add_rsqrt_fusion.3, bf16[16384,128]{1,0:T(8,128)(2,1)} %param.11, f32[512,16384]{1,0:T(8,128)} %get-tuple-element.27, f32[512]{0:T(512)S(1)} %get-tuple-element.19, ...), kind=kOutput, calls=%fused_computation.28 | convolution fusion | flops 2181430784 | bytes 38543360 | tf_op jit(solution)/shard_map/dot_general | solution.py:58
  128.5 0.1 multiply_convert_fusion.2
  128.6 3.9 fusion.12
  132.5 5.3 fusion.25
  137.7 0.0 reduce-scatter.5.cloned.1.call-update
  137.7 0.0 reduce-scatter.7.cloned.1.call-start
  137.8 11.8 convolution_bitcast_fusion
  149.6 17.6 %copy.19 = f32[2048,2048]{1,0:T(8,128)} copy(f32[2048,2048]{0,1:T(8,128)} %convolution_bitcast_fusion) | data formatting | bytes 33554432
  167.2 0.0 reduce-scatter.7.cloned.1.call-update
  167.2 618.2 %reduce-scatter.5.cloned.1.call-done = f32[16,128]{1,0:T(8,128)} async-done(((f32[2048,128]{1,0:T(8,128)}), f32[16,128]{1,0:T(8,128)}) %reduce-scatter.5.cloned.1.call-update) | async-done | bytes 8208 | tf_op jit(solution)/shard_map/reduce_scatter | solution.py:114
  785.4 668.9 %reduce-scatter.7.cloned.1.call-done = f32[16,2048]{1,0:T(8,128)} async-done(((f32[2048,2048]{1,0:T(8,128)}), f32[16,2048]{1,0:T(8,128)}) %reduce-scatter.7.cloned.1.call-update) | async-done | bytes 131088
  (8 shorter events, 0.1 us)
Async XLA Ops:
  7.2 39.8 %copy-start = (bf16[512,2048]{1,0:T(8,128)(2,1)S(1)}, bf16[512,2048]{1,0:T(8,128)(2,1)}, u32[]{:S(2)}) copy-start(bf16[512,2048]{1,0:T(8,128)(2,1)} %param.8) | copy-start | bytes 6291460
  41.2 35.7 %all-to-all-start.1 = ((bf16[128,4,2048]{2,1,0:T(4,128)(2,1)}), bf16[128,4,2048]{2,1,0:T(4,128)(2,1)}, u32[]{:S(2)}, u32[]{:S(2)}) async-start(bf16[128,4,2048]{2,1,0:T(4,128)(2,1)} %reshape.116), calls=%async_computation.1 | async-start | bytes 4194304 | tf_op jit(solution)/shard_map/all_to_all | solution.py:97
  47.0 9.1 copy-start.2
  54.0 2.0 copy-start.1
  80.9 7.7 copy-start.3
  90.2 20.4 %all-to-all-start.2 = ((f32[128,4,128]{2,1,0:T(4,128)}), f32[128,4,128]{2,1,0:T(4,128)S(1)}, u32[]{:S(2)}, u32[]{:S(2)}) async-start(f32[128,4,128]{2,1,0:T(4,128)} %bitcast.2), calls=%async_computation.2 | async-start | bytes 524288 | tf_op jit(solution)/shard_map/all_to_all | solution.py:103
  94.8 690.6 %reduce-scatter.5.cloned.1.call-start = ((), (), s32[]{:S(2)}) async-start(), calls=%async_computation.5 | async-start | bytes 1056768 | tf_op jit(solution)/shard_map/reduce_scatter | solution.py:114
  137.7 1316.5 %reduce-scatter.7.cloned.1.call-start = ((), (), s32[]{:S(2)}) async-start(), calls=%async_computation.6 | async-start | bytes 16908288
Sparse Core Ops, SparseCore 0:
  137.9 647.5 reduce-scatter.4
  788.4 665.8 reduce-scatter.6
where the time goes:
time: 1460 us
  waiting for transfers between devices  1310 us (90%)
  matrix products  68.7 us (5%)
  local copies, waits for them, and re-layouts  37.5 us (3%)
  blocking collectives  20.3 us (1%)
    unnamed x3, waiting for transfers between devices  669 us
    reduce_scatter x1, waiting for transfers between devices, per_device(): lax.psum_scatter(grad_out, ('dp', 'crop'), scatter_dimension=0, tiled=True)  618 us
  transfers between devices with their start and end apart: 4, of which 3 were waited for; matrix products, arithmetic and copies ran while one was open for 4% of the time, Pallas kernels for 0%

commit v1 on v0

--- a/solution.py
+++ b/solution.py
@@ -109,10 +109,15 @@
     grad_in, grad_out = query_grads(
         query_crops, matching_targets, distractor_bank, query_inner, query_outer, all_rows
     )
-    grad_in, grad_out = (
-        lax.psum_scatter(grad_in, ("dp", "crop"), scatter_dimension=0, tiled=True),
-        lax.psum_scatter(grad_out, ("dp", "crop"), scatter_dimension=0, tiled=True),
+    width_in, width_out = grad_in.shape[1], grad_out.shape[1]
+    slices = (
+        jnp.concatenate([grad_in, grad_out], axis=1)
+        .astype(jnp.bfloat16)
+        .reshape(group_count, grad_in.shape[0] // group_count, width_in + width_out)
     )
+    partials = lax.all_to_all(slices, ("dp", "crop"), split_axis=0, concat_axis=0, tiled=True)
+    summed = jnp.sum(partials.astype(jnp.float32), axis=0)
+    grad_in, grad_out = summed[:, :width_in], summed[:, width_in:]
     return (grad_in, grad_out)
 
 

time: 1460 us -> 259 us (0.18)
  waiting for transfers between devices: 1310 us -> 20 us
  blocking collectives: 20.3 us -> 134 us
  local copies, waits for them, and re-layouts: 37.5 us -> 21.4 us
    unnamed x3 -> x0, waiting for transfers between devices: 669 us -> none
    reduce_scatter x1 -> x0, waiting for transfers between devices: 618 us -> none  [per_device(): lax.psum_scatter(grad_out, ('dp', 'crop'), scatter_dimension=0, tiled=True)]
    all_to_all x0 -> x1, blocking collectives: none -> 114 us  [per_device(): lax.all_to_all(slices, ('dp', 'crop'), split_axis=0, concat_axis=0, tiled...]
    unnamed x9 -> x10, local copies, waits for them, and re-layouts: 19.6 us -> 2.3 us
  transfers between devices with their start and end apart: 4 -> 2, of which waited for: 3 -> 1; matrix products, arithmetic and copies ran while one was open for 4% -> 9% of each run, Pallas kernels for 0% -> 0%
where the time goes in v1:
time: 259 us; the launch traced here: 257 us
  blocking collectives  134 us (52%)
  matrix products  59 us (23%)
  local copies, waits for them, and re-layouts  21.4 us (8%)
  waiting for transfers between devices  20 us (8%)
  other arithmetic  11.8 us (5%)
  starting transfers between devices  10.5 us (4%)
    all_to_all x1, blocking collectives, per_device(): lax.all_to_all(slices, ('dp', 'crop'), split_axis=0, concat_axis=0, tiled...  114 us
    all_to_all x1, blocking collectives, per_device(): lax.all_to_all(wanted, ('dp', 'crop'), split_axis=0, concat_axis=0, tiled...  20.3 us
    all_to_all x1, waiting for transfers between devices, per_device(): lax.all_to_all(outgoing, ('dp', 'crop'), split_axis=0, concat_axis=0, til...  20 us
    dot_general x1, matrix products, query_grads(): jnp.dot(distractor_similarity_slope, distractor_bank, preferred_element_t...  15.9 us
    dot_general x1, matrix products, query_grads(): lax.dot_general(probe_features.astype(jnp.bfloat16), distractor_bank, (((...  15.6 us
    concatenate x1, other arithmetic, per_device(): jnp.concatenate([grad_in, grad_out], axis=1).astype(jnp.bfloat16)  7.86 us
    dot_general x1, matrix products, key_embed(): hidden = jnp.dot(crop_rows, w_in, preferred_element_type=jnp.float32)  7.66 us
    gather x1, local copies, waits for them, and re-layouts, per_device(): key_crops[flat_req].reshape(group_count, per_peer, key_crops.shape[1])  7.15 us
  transfers between devices with their start and end apart: 2, of which 1 were waited for; matrix products, arithmetic and copies ran while one was open for 9% of the time, Pallas kernels for 0%

profile of v1, /device:TPU:0, one launch (start us, length us, event | category | flops | bytes accessed | tf_op | source)
XLA Modules:
  0.0 257.5 jit_solution(10690965976407097805)
XLA Ops:
  0.6 0.0 copy-start
  0.6 0.8 add_select_fusion
  1.5 0.1 all_to_all.15
  1.6 20.3 %all_to_all.24 = s32[128,1,4]{2,1,0:T(1,128)S(1)} all-to-all(s32[128,1,4]{2,1,0:T(1,128)S(1)} %bitcast.24), channel_id=1, replica_groups=mesh['dp'=32,'crop'=4] {'dp','crop'}, dimensions={0} | all-to-all | bytes 4096 | tf_op jit(solution)/shard_map/all_to_all | solution.py:94
  21.9 0.5 broadcast.154
  22.4 0.8 reduce.3
  23.2 0.1 reshape.120
  23.4 7.2 %gather_fusion = bf16[512,2048]{1,0:T(8,128)(2,1)} fusion(bf16[512,2048]{1,0:T(8,128)(2,1)} %param.9, s32[1024]{0:T(1024)S(1)} %pad_clamp_fusion), kind=kCustom, calls=%fused_computation | custom fusion | bytes 4196352 | tf_op jit(solution)/shard_map/gather | solution.py:96
  30.5 4.1 %reshape.121 = bf16[128,4,2048]{2,1,0:T(4,128)(2,1)} reshape(bf16[512,2048]{1,0:T(8,128)(2,1)} %gather_fusion) | data formatting | bytes 4194304 | tf_op jit(solution)/shard_map/reshape | solution.py:96
  34.6 5.8 %all-to-all-start.1 = ((bf16[128,4,2048]{2,1,0:T(4,128)(2,1)}), bf16[128,4,2048]{2,1,0:T(4,128)(2,1)}, u32[]{:S(2)}, u32[]{:S(2)}) async-start(bf16[128,4,2048]{2,1,0:T(4,128)(2,1)} %reshape.121), calls=%async_computation.1 | async-start | bytes 4194304 | tf_op jit(solution)/shard_map/all_to_all | solution.py:97
  40.4 0.0 copy-done
  40.4 0.0 copy-start.3
  40.5 7.0 %multiply_reduce_fusion.2 = (f32[2048]{0:T(1024)S(1)}, f32[2048]{0:T(1024)S(1)}, f32[512,2048]{1,0:T(8,128)S(1)}) fusion(bf16[512,2048]{1,0:T(8,128)(2,1)S(1)} %copy-done, bf16[2048,2048]{1,0:T(8,128)(2,1)} %param.12), kind=kOutput, calls=%fused_computation.15 | convolution fusion | flops 4298108928 | bytes 14696448 | tf_op jit(solution)/shard_map/dot_general | solution.py:31
  47.5 0.0 copy-start.1
  47.5 2.0 copy-done.1
  49.5 0.0 copy-done.3
  49.5 0.8 multiply_reduce_fusion.6
  50.3 20.0 %all-to-all-done.1 = bf16[128,4,2048]{2,1,0:T(4,128)(2,1)} async-done(((bf16[128,4,2048]{2,1,0:T(4,128)(2,1)}), bf16[128,4,2048]{2,1,0:T(4,128)(2,1)}, u32[]{:S(2)}, u32[]{:S(2)}) %all-to-all-start.1) | async-done | bytes 2097184 | tf_op jit(solution)/shard_map/all_to_all | solution.py:97
  70.4 4.0 %reshape.122 = bf16[512,2048]{1,0:T(8,128)(2,1)} reshape(bf16[128,4,2048]{2,1,0:T(4,128)(2,1)} %all-to-all-done.1) | data formatting | bytes 4194304 | tf_op jit(solution)/shard_map/reshape | solution.py:99
  74.4 0.0 copy-start.4
  74.4 7.7 %fusion.25 = (f32[2048]{0:T(1024)S(1)}, f32[2048]{0:T(1024)S(1)}, f32[512,2048]{1,0:T(8,128)S(1)}) fusion(bf16[512,2048]{1,0:T(8,128)(2,1)} %reshape.122, bf16[2048,2048]{1,0:T(8,128)(2,1)} %param.14), kind=kOutput, calls=%fused_computation.63 | convolution fusion | flops 4298108928 | bytes 14696448 | tf_op jit(solution)/shard_map/dot_general | solution.py:25
  82.0 0.0 copy-done.4
  82.0 0.8 multiply_reduce_fusion.5
  82.9 0.9 broadcast_multiply_fusion
  83.7 4.7 %all-to-all-start.2 = ((f32[128,4,128]{2,1,0:T(4,128)}), f32[128,4,128]{2,1,0:T(4,128)S(1)}, u32[]{:S(2)}, u32[]{:S(2)}) async-start(f32[128,4,128]{2,1,0:T(4,128)} %bitcast.2), calls=%async_computation.2 | async-start | bytes 524288 | tf_op jit(solution)/shard_map/all_to_all | solution.py:103
  88.5 15.6 %fusion = (f32[512]{0:T(512)S(1)}, f32[512,16384]{1,0:T(8,128)}) fusion(bf16[16384,128]{1,0:T(8,128)(2,1)} %param.11, f32[512,128]{0,1:T(8,128)S(1)} %get-tuple-element.16, f32[512]{0:T(512)S(1)} %add_rsqrt_fusion.3), kind=kOutput, calls=%fused_computation.4 | convolution fusion | flops 2164391424 | bytes 38014976 | tf_op jit(solution)/shard_map/dot_general | solution.py:42
  104.0 0.0 all-to-all-done.2
  104.0 1.8 scatter_custom_fusion
  105.8 0.1 copy.14
  106.0 0.1 multiply_reduce_fusion.4
  106.0 15.9 %multiply_reduce_fusion.3 = (f32[512]{0:T(512)S(1)}, f32[512,128]{0,1:T(8,128)S(1)}) fusion(f32[512,128]{0,1:T(8,128)S(1)} %get-tuple-element.16, f32[512]{0:T(512)S(1)} %add_rsqrt_fusion.3, bf16[16384,128]{1,0:T(8,128)(2,1)} %param.11, f32[512,16384]{1,0:T(8,128)} %get-tuple-element.21, f32[512]{0:T(512)S(1)} %get-tuple-element.13, ...), kind=kOutput, calls=%fused_computation.30 | convolution fusion | flops 2181430784 | bytes 38543360 | tf_op jit(solution)/shard_map/dot_general | solution.py:58
  121.9 0.0 copy-start.2
  121.9 0.1 multiply_convert_fusion.2
  122.0 3.1 %convolution_convert_fusion.1 = bf16[2048,128]{1,0:T(8,128)(2,1)S(1)} fusion(bf16[512,128]{0,1:T(8,128)(2,1)S(1)} %multiply_convert_fusion.2, f32[512,2048]{1,0:T(8,128)} %copy-done.1, f32[2048]{0:T(1024)S(1)} %get-tuple-element.11, f32[2048]{0:T(1024)S(1)} %get-tuple-element.10), kind=kOutput, calls=%fused_computation.17 | convolution fusion | flops 272891904 | bytes 4866048 | tf_op jit(solution)/shard_map/dot_general | solution.py:67
  125.1 0.3 copy-done.2
  125.4 1.1 fusion.24
  126.5 7.0 %convolution_convert_fusion = bf16[2048,2048]{0,1:T(8,128)(2,1)} fusion(bf16[512,2048]{1,0:T(8,128)(2,1)S(1)} %copy-done, f32[512,2048]{1,0:T(8,128)S(1)} %get-tuple-element.24, f32[512,2048]{1,0:T(8,128)S(1)} %copy-done.2, f32[2048]{0:T(1024)S(1)} %get-tuple-element.25, f32[2048]{0:T(1024)S(1)} %get-tuple-element.26, f32[2048]{0:T(1024)S(1)} %get-tuple-element.11, ...), kind=kOutput, calls=%fused_computation.8 | convolution fusion | flops 4306501632 | bytes 18907136 | tf_op jit(solution)/shard_map/dot_general | solution.py:77
  133.5 7.9 %pad_maximum_fusion = bf16[128,16,2176]{2,1,0:T(8,128)(2,1)} fusion(bf16[128,16,128]{2,1,0:T(8,128)(2,1)S(1)} %bitcast.22, bf16[128,16,2048]{2,1,0:T(8,128)(2,1)} %bitcast.21), kind=kLoop, calls=%fused_computation.7 | loop fusion | flops 17825792 | bytes 17825792 | tf_op jit(solution)/shard_map/concatenate | solution.py:114
  141.4 113.6 %all_to_all.25 = bf16[128,16,2176]{2,1,0:T(8,128)(2,1)S(1)} all-to-all(bf16[128,16,2176]{2,1,0:T(8,128)(2,1)} %pad_maximum_fusion), channel_id=1, replica_groups=mesh['dp'=32,'crop'=4] {'dp','crop'}, dimensions={0} | all-to-all | bytes 17825792 | tf_op jit(solution)/shard_map/all_to_all | solution.py:118
  255.0 1.2 convert_reduce_fusion
  256.2 0.6 slice.11
  256.8 0.7 slice.10
  (8 shorter events, 0.1 us)
Async XLA Ops:
  0.6 39.8 %copy-start = (bf16[512,2048]{1,0:T(8,128)(2,1)S(1)}, bf16[512,2048]{1,0:T(8,128)(2,1)}, u32[]{:S(2)}) copy-start(bf16[512,2048]{1,0:T(8,128)(2,1)} %param.8) | copy-start | bytes 6291460
  34.6 35.7 %all-to-all-start.1 = ((bf16[128,4,2048]{2,1,0:T(4,128)(2,1)}), bf16[128,4,2048]{2,1,0:T(4,128)(2,1)}, u32[]{:S(2)}, u32[]{:S(2)}) async-start(bf16[128,4,2048]{2,1,0:T(4,128)(2,1)} %reshape.121), calls=%async_computation.1 | async-start | bytes 4194304 | tf_op jit(solution)/shard_map/all_to_all | solution.py:97
  40.4 9.1 %copy-start.3 = (bf16[2048,128]{1,0:T(8,128)(2,1)S(1)}, bf16[2048,128]{1,0:T(8,128)(2,1)}, u32[]{:S(2)}) copy-start(bf16[2048,128]{1,0:T(8,128)(2,1)} %param.13) | copy-start | bytes 1572868
  47.5 2.0 copy-start.1
  74.4 7.7 %copy-start.4 = (bf16[2048,128]{1,0:T(8,128)(2,1)S(1)}, bf16[2048,128]{1,0:T(8,128)(2,1)}, u32[]{:S(2)}) copy-start(bf16[2048,128]{1,0:T(8,128)(2,1)} %param.15) | copy-start | bytes 1572868
  83.7 20.3 %all-to-all-start.2 = ((f32[128,4,128]{2,1,0:T(4,128)}), f32[128,4,128]{2,1,0:T(4,128)S(1)}, u32[]{:S(2)}, u32[]{:S(2)}) async-start(f32[128,4,128]{2,1,0:T(4,128)} %bitcast.2), calls=%async_computation.2 | async-start | bytes 524288 | tf_op jit(solution)/shard_map/all_to_all | solution.py:103
  121.9 3.5 %copy-start.2 = (f32[512,2048]{1,0:T(8,128)S(1)}, f32[512,2048]{1,0:T(8,128)}, u32[]{:S(2)}) copy-start(f32[512,2048]{1,0:T(8,128)} %copy-done.1) | copy-start | bytes 12582916

commit v2 on v0

--- a/solution.py
+++ b/solution.py
@@ -1,12 +1,221 @@
+import functools
 import jax
 import jax.numpy as jnp
 from jax import lax
+from jax.experimental import pallas as pl
+from jax.experimental.pallas import tpu as pltpu
 from jax.sharding import PartitionSpec as P
 
 sharpness_divisor = 0.2
 loss_scale = 4096.0
 bn_eps = 1e-05
 norm_eps = 1e-06
+
+
+MESH = pl.DeviceIdType.MESH
+CHUNK = 16
+LANES = 128
+TURNS = (("x", 1), ("y", 1), ("z", 1), ("x", 3), ("y", 3), ("z", 3))
+AXES = ("x", "y", "z")
+
+
+def place():
+    dp, crop = lax.axis_index("dp"), lax.axis_index("crop")
+    return {
+        "x": dp // 8,
+        "z": (dp // 2) % 4,
+        "y": (dp % 2) * 2 + crop // 2,
+        "core": crop % 2,
+    }
+
+
+def device_of(at):
+    return (at["x"] * 8 + at["z"] * 2 + at["y"] // 2, (at["y"] % 2) * 2 + at["core"])
+
+
+def mirrored(v, u):
+    return (v, v + 1 - 2 * (v % 2), (v + 2) % 4, 3 - v)[u]
+
+
+def partner(at, turn):
+    if turn is None:
+        return device_of({**at, "core": 1 - at["core"]})
+    axis, flip = turn
+    return device_of({**at, axis: mirrored(at[axis], flip)})
+
+
+def greet(at):
+    barrier = pltpu.get_barrier_semaphore()
+    for turn in (None,) + TURNS:
+        pl.semaphore_signal(barrier, inc=1, device_id=partner(at, turn), device_id_type=MESH)
+    pl.semaphore_wait(barrier, 1 + len(TURNS))
+
+
+def plan_of(kind):
+    held = {a: [0, 1, 2, 3] for a in AXES}
+    hops = []
+    for k in range(6):
+        axis, flip = TURNS[(kind + k) % 6]
+        now = held[axis]
+        if len(now) == 4:
+            sent = [1, 2] if flip == 1 else [3, 2]
+        else:
+            sent = [flip]
+        kept = [u ^ flip for u in sent]
+        dims = tuple(len(held[a]) for a in AXES)
+        hops.append(
+            (dims, AXES.index(axis), [now.index(u) for u in kept], [now.index(u) for u in sent])
+        )
+        held[axis] = kept
+    return hops
+
+
+PLANS = [plan_of(kind) for kind in range(6)]
+
+
+def grads_kernel(tiles, xt_ref, dh_ref, go_ref, gi_out, go_out, xp, *rest):
+    acc, send, recv = rest[0:7], rest[7:14], rest[14:21]
+    send_sem, recv_sem = rest[21], rest[22]
+    slots = tiles + 2
+    at = place()
+    greet(at)
+
+    def copy(k, t, kind):
+        turn = None if k == 0 else TURNS[(kind + k - 1) % 6]
+        return pltpu.make_async_remote_copy(
+            src_ref=send[k].at[t],
+            dst_ref=recv[k].at[t],
+            send_sem=send_sem.at[k, t],
+            recv_sem=recv_sem.at[k, t],
+            device_id=partner(at, turn),
+            device_id_type=MESH,
+        )
+
+    def combine(k, t, kind):
+        copy(k, t, kind).wait_recv()
+        total = acc[k][t] + recv[k][t].astype(jnp.float32)
+        if k == 6:
+            return total[0]
+        dims, axis, kept, sent = PLANS[kind][k]
+        total = total.reshape(dims + (CHUNK, LANES))
+        out_dims = tuple(n // 2 if i == axis else n for i, n in enumerate(dims))
+
+        def pick(positions):
+            parts = [lax.slice_in_dim(total, p, p + 1, axis=axis) for p in positions]
+            joined = parts[0] if len(parts) == 1 else jnp.concatenate(parts, axis=axis)
+            return joined.reshape((-1, CHUNK, LANES))
+
+        send[k + 1][t] = pick(sent).astype(jnp.bfloat16)
+        acc[k + 1][t] = pick(kept)
+        copy(k + 1, t, kind).start()
+
+    rows = {}
+    index = 0
+    for far in (1, 0):
+        core = at["core"] if far == 0 else 1 - at["core"]
+        for ux in range(4):
+            for uy in range(4):
+                for uz in range(4):
+                    wx, wy, wz = (mirrored(at[a], u) for a, u in zip(AXES, (ux, uy, uz)))
+                    row = pl.multiple_of((((wx * 4 + wz) * 4 + wy) * 2 + core) * CHUNK, CHUNK)
+                    rows[index] = row
+                    xp[index * CHUNK : (index + 1) * CHUNK, :] = xt_ref[pl.ds(row, CHUNK), :]
+                    index += 1
+
+    def outer():
+        for i in range(64):
+            send[0][tiles, i] = go_ref[pl.ds(rows[i], CHUNK), :].astype(jnp.bfloat16)
+            acc[0][tiles, i] = go_ref[pl.ds(rows[64 + i], CHUNK), :]
+        send[0][tiles + 1] = jnp.zeros((64, CHUNK, LANES), jnp.bfloat16)
+        acc[0][tiles + 1] = jnp.zeros((64, CHUNK, LANES), jnp.float32)
+        for t in (tiles, tiles + 1):
+            copy(0, t, t % 6).start()
+
+    def inner(g):
+        right = dh_ref[:, 2 * g * LANES : (2 * g + 2) * LANES]
+
+        def block(far, b):
+            left = xp[pl.ds(pl.multiple_of((far * 4 + b) * 256, 256), 256), :]
+            part = jnp.dot(left, right, preferred_element_type=jnp.float32)
+            for h in range(2):
+                half = part[:, h * LANES : (h + 1) * LANES].reshape(16, CHUNK, LANES)
+                where = pl.ds(b * 16, 16)
+                if far == 0:
+                    send[0][2 * g + h, where] = half.astype(jnp.bfloat16)
+                else:
+                    acc[0][2 * g + h, where] = half
+
+        @pl.loop(0, 4)
+        def _(b):
+            block(0, b)
+
+        for h in range(2):
+            copy(0, 2 * g + h, (2 * g + h) % 6).start()
+
+        @pl.loop(0, 4)
+        def _(b):
+            block(1, b)
+
+    pairs = slots // 2
+    for g in range(pairs + 1):
+        if g < pairs - 1:
+            inner(g)
+        elif g == pairs - 1:
+            outer()
+        if g >= 1:
+            for h in range(2):
+                t = 2 * (g - 1) + h
+                combine(0, t, t % 6)
+
+    for k in range(1, 6):
+
+        @pl.loop(0, slots // 6)
+        def _(r, k=k):
+            for kind in range(6):
+                combine(k, r * 6 + kind, kind)
+
+    for t in range(slots - 1):
+        if t < tiles:
+            gi_out[:, t * LANES : (t + 1) * LANES] = combine(6, t, t % 6)
+        else:
+            go_out[...] = combine(6, t, t % 6)
+    combine(6, slots - 1, (slots - 1) % 6)
+
+    for k in range(7):
+
+        @pl.loop(0, slots // 6)
+        def _(r, k=k):
+            for kind in range(6):
+                copy(k, r * 6 + kind, kind).wait_send()
+
+
+def summed_grads(crops_t, d_hidden, grad_outer):
+    depth, batch = crops_t.shape
+    width = d_hidden.shape[1]
+    tiles = width // LANES
+    slots = tiles + 2
+
+    def slabs(dtype):
+        return [pltpu.VMEM((slots, 64 >> k, CHUNK, LANES), dtype) for k in range(7)]
+
+    return pl.pallas_call(
+        functools.partial(grads_kernel, tiles),
+        out_shape=(
+            jax.ShapeDtypeStruct((CHUNK, width), jnp.float32),
+            jax.ShapeDtypeStruct((CHUNK, LANES), jnp.float32),
+        ),
+        in_specs=[pl.BlockSpec(memory_space=pltpu.VMEM)] * 3,
+        out_specs=[pl.BlockSpec(memory_space=pltpu.VMEM)] * 2,
+        scratch_shapes=[pltpu.VMEM((depth, batch), jnp.bfloat16)]
+        + slabs(jnp.float32)
+        + [pltpu.VMEM((slots, 64, CHUNK, LANES), jnp.bfloat16)]
+        + slabs(jnp.bfloat16)[1:]
+        + slabs(jnp.bfloat16)
+        + [pltpu.SemaphoreType.DMA((7, slots)), pltpu.SemaphoreType.DMA((7, slots))],
+        compiler_params=pltpu.CompilerParams(
+            collective_id=0, has_side_effects=True, vmem_limit_bytes=60 << 20
+        ),
+    )(crops_t, d_hidden, grad_outer)
 
 
 def batch_stats(hidden):
@@ -74,13 +283,7 @@
     d_hidden = inv_std * (
         d_norm - jnp.mean(d_norm, axis=0) - normed * jnp.mean(d_norm * normed, axis=0)
     )
-    grad_in = lax.dot_general(
-        crop_rows,
-        d_hidden.astype(jnp.bfloat16),
-        (((0,), (0,)), ((), ())),
-        preferred_element_type=jnp.float32,
-    )
-    return (grad_in, grad_out)
+    return summed_grads(crop_rows.T, d_hidden.astype(jnp.bfloat16), grad_out)
 
 
 def per_device(
@@ -109,10 +312,6 @@
     grad_in, grad_out = query_grads(
         query_crops, matching_targets, distractor_bank, query_inner, query_outer, all_rows
     )
-    grad_in, grad_out = (
-        lax.psum_scatter(grad_in, ("dp", "crop"), scatter_dimension=0, tiled=True),
-        lax.psum_scatter(grad_out, ("dp", "crop"), scatter_dimension=0, tiled=True),
-    )
     return (grad_in, grad_out)
 
 

time: 1460 us -> 180 us (0.12)
  waiting for transfers between devices: 1310 us -> 19.8 us
  Pallas kernels: 0 us -> 50.8 us
  local copies, waits for them, and re-layouts: 37.5 us -> 19.5 us
  matrix products: 68.7 us -> 53.8 us
    unnamed x3 -> x0, waiting for transfers between devices: 669 us -> none
    reduce_scatter x1 -> x0, waiting for transfers between devices: 618 us -> none  [per_device(): lax.psum_scatter(grad_out, ('dp', 'crop'), scatter_dimension=0, tiled=True)]
    pallas_call x0 -> x1, Pallas kernels: none -> 50.8 us  [summed_grads(): pl.pallas_call(functools.partial(grads_kernel, tiles), out_shape=(jax.Sha...]
  transfers between devices with their start and end apart: 4 -> 2, of which waited for: 3 -> 1; matrix products, arithmetic and copies ran while one was open for 4% -> 15% of each run, Pallas kernels for 0% -> 0%
where the time goes in v2:
time: 180 us
  matrix products  53.8 us (30%)
  Pallas kernels  50.8 us (28%)
  blocking collectives  20.3 us (11%)
  waiting for transfers between devices  19.8 us (11%)
  local copies, waits for them, and re-layouts  19.5 us (11%)
  starting transfers between devices  9.54 us (5%)
  other arithmetic  5.16 us (3%)
    pallas_call x1, Pallas kernels, summed_grads(): pl.pallas_call(functools.partial(grads_kernel, tiles), out_shape=(jax.Sha...  50.8 us
    all_to_all x1, blocking collectives, per_device(): lax.all_to_all(wanted, ('dp', 'crop'), split_axis=0, concat_axis=0, tiled...  20.3 us
    all_to_all x1, waiting for transfers between devices, per_device(): lax.all_to_all(outgoing, ('dp', 'crop'), split_axis=0, concat_axis=0, til...  19.8 us
    dot_general x1, matrix products, query_grads(): jnp.dot(distractor_similarity_slope, distractor_bank, preferred_element_t...  15.9 us
    dot_general x1, matrix products, query_grads(): lax.dot_general(probe_features.astype(jnp.bfloat16), distractor_bank, (((...  15.7 us
    dot_general x1, matrix products, query_grads(): hidden = jnp.dot(crop_rows, w_in, preferred_element_type=jnp.float32)  7.67 us
    dot_general x1, matrix products, key_embed(): hidden = jnp.dot(crop_rows, w_in, preferred_element_type=jnp.float32)  7.66 us
    unnamed x17, local copies, waits for them, and re-layouts  7.42 us
  transfers between devices with their start and end apart: 2, of which 1 were waited for; matrix products, arithmetic and copies ran while one was open for 15% of the time, Pallas kernels for 0%

profile of v2, /device:TPU:0, one launch (start us, length us, event | category | flops | bytes accessed | tf_op | source)
XLA Modules:
  0.0 179.8 jit_solution(10588261909658096688)
XLA Ops:
  0.6 0.0 copy-start
  0.6 0.8 add_select_fusion
  1.5 0.1 all_to_all.12
  1.6 20.3 %all_to_all.19 = s32[128,1,4]{2,1,0:T(1,128)S(1)} all-to-all(s32[128,1,4]{2,1,0:T(1,128)S(1)} %bitcast.18), channel_id=1, replica_groups=mesh['dp'=32,'crop'=4] {'dp','crop'}, dimensions={0} | all-to-all | bytes 4096 | tf_op jit(solution)/shard_map/all_to_all | solution.py:297
  21.9 0.5 broadcast.154
  22.4 0.8 reduce.3
  23.2 0.1 reshape.115
  23.4 0.0 copy-done
  23.4 3.3 %gather_fusion = bf16[512,2048]{1,0:T(8,128)(2,1)} fusion(bf16[512,2048]{1,0:T(8,128)(2,1)S(1)} %copy-done, s32[1024]{0:T(1024)S(1)} %pad_clamp_fusion), kind=kCustom, calls=%fused_computation | custom fusion | bytes 4196352 | tf_op jit(solution)/shard_map/gather | solution.py:299
  26.7 4.1 %reshape.116 = bf16[128,4,2048]{2,1,0:T(4,128)(2,1)} reshape(bf16[512,2048]{1,0:T(8,128)(2,1)} %gather_fusion) | data formatting | bytes 4194304 | tf_op jit(solution)/shard_map/reshape | solution.py:299
  30.8 4.8 %all-to-all-start.1 = ((bf16[128,4,2048]{2,1,0:T(4,128)(2,1)}), bf16[128,4,2048]{2,1,0:T(4,128)(2,1)S(1)}, u32[]{:S(2)}, u32[]{:S(2)}) async-start(bf16[128,4,2048]{2,1,0:T(4,128)(2,1)} %reshape.116), calls=%async_computation.1 | async-start | bytes 4194304 | tf_op jit(solution)/shard_map/all_to_all | solution.py:300
  35.6 0.0 copy-start.4
  35.6 7.7 %multiply_reduce_fusion.2 = (f32[2048]{0:T(1024)S(1)}, f32[2048]{0:T(1024)S(1)}, f32[512,2048]{1,0:T(8,128)S(1)}) fusion(bf16[512,2048]{1,0:T(8,128)(2,1)} %param.8, bf16[2048,2048]{1,0:T(8,128)(2,1)} %param.12), kind=kOutput, calls=%fused_computation.12 | convolution fusion | flops 4298108928 | bytes 14696448 | tf_op jit(solution)/shard_map/dot_general | solution.py:240
  43.3 0.0 copy-start.2
  43.3 2.0 %copy-done.2 = f32[512,2048]{1,0:T(8,128)} copy-done((f32[512,2048]{1,0:T(8,128)}, f32[512,2048]{1,0:T(8,128)S(1)}, u32[]{:S(2)}) %copy-start.2) | copy-done | bytes 4194328
  45.3 0.0 copy-done.4
  45.3 0.8 multiply_reduce_fusion.6
  46.2 19.8 %all-to-all-done.1 = bf16[128,4,2048]{2,1,0:T(4,128)(2,1)S(1)} async-done(((bf16[128,4,2048]{2,1,0:T(4,128)(2,1)}), bf16[128,4,2048]{2,1,0:T(4,128)(2,1)S(1)}, u32[]{:S(2)}, u32[]{:S(2)}) %all-to-all-start.1) | async-done | bytes 2097184 | tf_op jit(solution)/shard_map/all_to_all | solution.py:300
  66.0 2.1 %reshape.117 = bf16[512,2048]{1,0:T(8,128)(2,1)} reshape(bf16[128,4,2048]{2,1,0:T(4,128)(2,1)S(1)} %all-to-all-done.1) | data formatting | bytes 4194304 | tf_op jit(solution)/shard_map/reshape | solution.py:302
  68.0 0.0 copy-start.6
  68.0 7.7 %fusion.22 = (f32[2048]{0:T(1024)S(1)}, f32[2048]{0:T(1024)S(1)}, f32[512,2048]{1,0:T(8,128)S(1)}) fusion(bf16[512,2048]{1,0:T(8,128)(2,1)} %reshape.117, bf16[2048,2048]{1,0:T(8,128)(2,1)} %param.14), kind=kOutput, calls=%fused_computation.56 | convolution fusion | flops 4298108928 | bytes 14696448 | tf_op jit(solution)/shard_map/dot_general | solution.py:234
  75.7 0.0 copy-done.6
  75.7 0.8 multiply_reduce_fusion.5
  76.5 0.9 broadcast_multiply_fusion
  77.4 4.7 %all-to-all-start.2 = ((f32[128,4,128]{2,1,0:T(4,128)}), f32[128,4,128]{2,1,0:T(4,128)S(1)}, u32[]{:S(2)}, u32[]{:S(2)}) async-start(f32[128,4,128]{2,1,0:T(4,128)} %bitcast.3), calls=%async_computation.2 | async-start | bytes 524288 | tf_op jit(solution)/shard_map/all_to_all | solution.py:306
  82.1 0.0 copy-start.5
  82.2 15.7 %fusion = (f32[512]{0:T(512)S(1)}, f32[512,16384]{1,0:T(8,128)}) fusion(bf16[16384,128]{1,0:T(8,128)(2,1)} %param.11, f32[512,128]{0,1:T(8,128)S(1)} %get-tuple-element.16, f32[512]{0:T(512)S(1)} %add_rsqrt_fusion.3), kind=kOutput, calls=%fused_computation.4 | convolution fusion | flops 2164391424 | bytes 38014976 | tf_op jit(solution)/shard_map/dot_general | solution.py:251
  97.9 0.0 copy-done.5
  97.9 2.5 %copy.15 = bf16[512,2048]{0,1:T(8,128)(2,1)} copy(bf16[512,2048]{1,0:T(8,128)(2,1)S(1)} %copy-done.5) | data formatting | bytes 4194304 | tf_op args[0]
  100.4 0.0 all-to-all-done.2
  100.4 1.8 scatter_custom_fusion
  102.2 0.1 copy.17
  102.3 0.1 multiply_reduce_fusion.4
  102.4 15.9 %multiply_reduce_fusion.3 = (f32[512]{0:T(512)S(1)}, f32[512,128]{0,1:T(8,128)S(1)}) fusion(f32[512,128]{0,1:T(8,128)S(1)} %get-tuple-element.16, f32[512]{0:T(512)S(1)} %add_rsqrt_fusion.3, bf16[16384,128]{1,0:T(8,128)(2,1)} %param.11, f32[512,16384]{1,0:T(8,128)} %get-tuple-element.21, f32[512]{0:T(512)S(1)} %get-tuple-element.13, ...), kind=kOutput, calls=%fused_computation.23 | convolution fusion | flops 2181430784 | bytes 38543360 | tf_op jit(solution)/shard_map/dot_general | solution.py:267
  118.3 0.0 copy-start.3
  118.3 0.1 multiply_convert_fusion.1
  118.3 4.1 %fusion.8.go_ref = f32[2048,128]{1,0:T(8,128)} fusion(bf16[512,128]{0,1:T(8,128)(2,1)S(1)} %multiply_convert_fusion.1, f32[512,2048]{1,0:T(8,128)} %copy-done.2, f32[2048]{0:T(1024)S(1)} %get-tuple-element.11, f32[2048]{0:T(1024)S(1)} %get-tuple-element.10), kind=kOutput, calls=%fused_computation.20 | convolution fusion | flops 272629760 | bytes 5390336 | tf_op jit(solution)/shard_map/dot_general | solution.py:276
  122.4 0.0 copy-done.3
  122.4 1.2 fusion.21
  123.6 0.0 copy-start.1
  123.6 2.5 %multiply_convert_fusion.dh_ref = bf16[512,2048]{1,0:T(8,128)(2,1)} fusion(f32[512,2048]{1,0:T(8,128)S(1)} %get-tuple-element.24, f32[512,2048]{1,0:T(8,128)S(1)} %copy-done.3, f32[2048]{0:T(1024)S(1)} %get-tuple-element.25, f32[2048]{0:T(1024)S(1)} %get-tuple-element.26, f32[2048]{0:T(1024)S(1)} %get-tuple-element.11, f32[2048]{0:T(1024)S(1)} %get-tuple-element.10), kind=kLoop, calls=%fused_computation.6 | loop fusion | flops 7340032 | bytes 10518528 | tf_op jit(solution)/shard_map/convert_element_type | solution.py:286
  126.1 50.8 %shard_map.95 = (f32[16,2048]{1,0:T(8,128)}, f32[16,128]{1,0:T(8,128)}) custom-call(bf16[2048,512]{1,0:T(8,128)(2,1)} %bitcast.16, bf16[512,2048]{1,0:T(8,128)(2,1)} %multiply_convert_fusion.dh_ref, f32[2048,128]{1,0:T(8,128)} %fusion.8.go_ref), custom_call_target="tpu_custom_call" | custom-call | tf_op jit(solution)/shard_map/pallas_call | solution.py:201
  176.9 1.6 copy.21
  178.5 1.3 copy.22
  179.8 0.0 copy-done.1
  (8 shorter events, 0.1 us)
Async XLA Ops:
  0.6 22.7 %copy-start = (bf16[512,2048]{1,0:T(8,128)(2,1)S(1)}, bf16[512,2048]{1,0:T(8,128)(2,1)}, u32[]{:S(2)}) copy-start(bf16[512,2048]{1,0:T(8,128)(2,1)} %param.9) | copy-start | bytes 6291460
  30.8 35.2 %all-to-all-start.1 = ((bf16[128,4,2048]{2,1,0:T(4,128)(2,1)}), bf16[128,4,2048]{2,1,0:T(4,128)(2,1)S(1)}, u32[]{:S(2)}, u32[]{:S(2)}) async-start(bf16[128,4,2048]{2,1,0:T(4,128)(2,1)} %reshape.116), calls=%async_computation.1 | async-start | bytes 4194304 | tf_op jit(solution)/shard_map/all_to_all | solution.py:300
  35.6 9.7 %copy-start.4 = (bf16[2048,128]{1,0:T(8,128)(2,1)S(1)}, bf16[2048,128]{1,0:T(8,128)(2,1)}, u32[]{:S(2)}) copy-start(bf16[2048,128]{1,0:T(8,128)(2,1)} %param.13) | copy-start | bytes 1572868
  43.3 2.0 %copy-start.2 = (f32[512,2048]{1,0:T(8,128)}, f32[512,2048]{1,0:T(8,128)S(1)}, u32[]{:S(2)}) copy-start(f32[512,2048]{1,0:T(8,128)S(1)} %get-tuple-element.14) | copy-start | bytes 12582916
  68.0 7.7 %copy-start.6 = (bf16[2048,128]{1,0:T(8,128)(2,1)S(1)}, bf16[2048,128]{1,0:T(8,128)(2,1)}, u32[]{:S(2)}) copy-start(bf16[2048,128]{1,0:T(8,128)(2,1)} %param.15) | copy-start | bytes 1572868
  77.4 23.0 %all-to-all-start.2 = ((f32[128,4,128]{2,1,0:T(4,128)}), f32[128,4,128]{2,1,0:T(4,128)S(1)}, u32[]{:S(2)}, u32[]{:S(2)}) async-start(f32[128,4,128]{2,1,0:T(4,128)} %bitcast.3), calls=%async_computation.2 | async-start | bytes 524288 | tf_op jit(solution)/shard_map/all_to_all | solution.py:306
  82.1 15.7 %copy-start.5 = (bf16[512,2048]{1,0:T(8,128)(2,1)S(1)}, bf16[512,2048]{1,0:T(8,128)(2,1)}, u32[]{:S(2)}) copy-start(bf16[512,2048]{1,0:T(8,128)(2,1)} %param.8) | copy-start | bytes 6291460
  118.3 4.2 %copy-start.3 = (f32[512,2048]{1,0:T(8,128)S(1)}, f32[512,2048]{1,0:T(8,128)}, u32[]{:S(2)}) copy-start(f32[512,2048]{1,0:T(8,128)} %copy-done.2) | copy-start | bytes 12582916
  123.6 56.1 %copy-start.1 = (bf16[512,2048]{1,0:T(8,128)(2,1)S(1)}, bf16[512,2048]{1,0:T(8,128)(2,1)}, u32[]{:S(2)}) copy-start(bf16[512,2048]{1,0:T(8,128)(2,1)} %param.9) | copy-start | bytes 6291460

commit v3 on v2

--- a/solution.py
+++ b/solution.py
@@ -1,4 +1,5 @@
 import functools
+import math
 import jax
 import jax.numpy as jnp
 from jax import lax
@@ -10,6 +11,7 @@
 loss_scale = 4096.0
 bn_eps = 1e-05
 norm_eps = 1e-06
+EXP2_SCALE = math.log2(math.e) / sharpness_divisor
 
 
 MESH = pl.DeviceIdType.MESH
@@ -218,6 +220,45 @@
     )(crops_t, d_hidden, grad_outer)
 
 
+def negatives_kernel(chunk, q_ref, bank_ref, total_ref, pull_ref):
+    @pl.when(pl.program_id(0) == 0)
+    def _():
+        total_ref[...] = jnp.zeros_like(total_ref)
+        pull_ref[...] = jnp.zeros_like(pull_ref)
+
+    keys = bank_ref[...]
+    for start in range(0, q_ref.shape[0], chunk):
+        rows = slice(start, start + chunk)
+        sims = lax.dot_general(
+            q_ref[rows, :].astype(jnp.bfloat16), keys, (((1,), (1,)), ((), ())), preferred_element_type=jnp.float32
+        )
+        quarter = jnp.exp2(sims * EXP2_SCALE - 2.0)
+        partial = quarter[:, 0:LANES]
+        for c in range(LANES, quarter.shape[1], LANES):
+            partial = partial + quarter[:, c : c + LANES]
+        total_ref[rows, :] += partial
+        pull_ref[rows, :] += jnp.dot(
+            quarter.astype(jnp.bfloat16), keys, preferred_element_type=jnp.float32
+        )
+
+
+def negatives(probe_features, distractor_bank, block=4096, chunk=256):
+    rows, emb = probe_features.shape
+    keys = distractor_bank.shape[0]
+    whole = pl.BlockSpec((rows, emb), lambda i: (0, 0))
+    return pl.pallas_call(
+        functools.partial(negatives_kernel, chunk),
+        grid=(keys // block,),
+        out_shape=(jax.ShapeDtypeStruct((rows, emb), jnp.float32),) * 2,
+        in_specs=[whole, pl.BlockSpec((block, emb), lambda i: (i, 0))],
+        out_specs=[whole, whole],
+        cost_estimate=pl.CostEstimate(
+            flops=4 * rows * keys * emb, bytes_accessed=2 * keys * emb, transcendentals=rows * keys
+        ),
+        compiler_params=pltpu.CompilerParams(vmem_limit_bytes=60 << 20),
+    )(probe_features, distractor_bank)
+
+
 def batch_stats(hidden):
     average = jnp.mean(hidden, axis=0)
     variance = jnp.mean(hidden * hidden, axis=0) - average * average
@@ -236,35 +277,27 @@
     return head_tail((hidden - average) * inv_std, w_out)
 
 
-def query_grads(crop_rows, matching_targets, distractor_bank, w_in, w_out, all_rows):
+def query_forward(crop_rows, w_in, w_out):
     hidden = jnp.dot(crop_rows, w_in, preferred_element_type=jnp.float32)
     average, inv_std = batch_stats(hidden)
     normed = (hidden - average) * inv_std
     active = jnp.maximum(normed, 0.0).astype(jnp.bfloat16)
     projected = jnp.dot(active, w_out, preferred_element_type=jnp.float32)
     inv_len = lax.rsqrt(jnp.sum(projected * projected, axis=-1, keepdims=True) + norm_eps)
-    probe_features = projected * inv_len
+    return (normed, active, inv_std, inv_len, projected * inv_len)
+
+
+def query_grads(crops_t, forward, lane_totals, pull, matching_targets, w_out, all_rows):
+    normed, active, inv_std, inv_len, probe_features = forward
     matching_similarity = (
         jnp.sum(probe_features * matching_targets, axis=-1, keepdims=True) / sharpness_divisor
     )
-    distractor_similarities = (
-        lax.dot_general(
-            probe_features.astype(jnp.bfloat16),
-            distractor_bank,
-            (((1,), (1,)), ((), ())),
-            preferred_element_type=jnp.float32,
-        )
-        / sharpness_divisor
-    )
-    exp_pos = jnp.exp(matching_similarity)
-    exp_neg = jnp.exp(distractor_similarities)
-    total_exp = exp_pos + jnp.sum(exp_neg, axis=-1, keepdims=True)
+    exp_pos = jnp.exp(matching_similarity) * 0.25
+    total_exp = exp_pos + jnp.sum(lane_totals, axis=-1, keepdims=True)
     scale_coef = loss_scale / all_rows
     matching_similarity_slope = scale_coef * (exp_pos / total_exp - 1.0)
-    distractor_similarity_slope = (scale_coef * exp_neg / total_exp).astype(jnp.bfloat16)
     probe_feature_slope = (
-        matching_similarity_slope * matching_targets
-        + jnp.dot(distractor_similarity_slope, distractor_bank, preferred_element_type=jnp.float32)
+        matching_similarity_slope * matching_targets + scale_coef * pull / total_exp
     ) / sharpness_divisor
     d_proj = (
         (
@@ -283,7 +316,7 @@
     d_hidden = inv_std * (
         d_norm - jnp.mean(d_norm, axis=0) - normed * jnp.mean(d_norm * normed, axis=0)
     )
-    return summed_grads(crop_rows.T, d_hidden.astype(jnp.bfloat16), grad_out)
+    return summed_grads(crops_t, d_hidden.astype(jnp.bfloat16), grad_out)
 
 
 def per_device(
@@ -297,22 +330,25 @@
     requested = lax.all_to_all(wanted, ("dp", "crop"), split_axis=0, concat_axis=0, tiled=True)
     flat_req = requested.reshape(-1)
     outgoing = key_crops[flat_req].reshape(group_count, per_peer, key_crops.shape[1])
-    incoming = lax.all_to_all(
-        outgoing, ("dp", "crop"), split_axis=0, concat_axis=0, tiled=True
-    ).reshape(row_count, key_crops.shape[1])
-    embedded = key_embed(incoming, key_inner, key_outer).reshape(
-        group_count, per_peer, key_outer.shape[1]
-    )
+    incoming = lax.all_to_all(outgoing, ("dp", "crop"), split_axis=0, concat_axis=0, tiled=True)
+    forward = query_forward(query_crops, query_inner, query_outer)
+    crops_t = query_crops.T
+    lane_totals, pull = negatives(forward[4], distractor_bank)
+    incoming, lane_totals, pull, crops_t = lax.optimization_barrier(
+        (incoming, lane_totals, pull, crops_t)
+    )
+    embedded = key_embed(
+        incoming.reshape(row_count, key_crops.shape[1]), key_inner, key_outer
+    ).reshape(group_count, per_peer, key_outer.shape[1])
     returned = lax.all_to_all(
         embedded, ("dp", "crop"), split_axis=0, concat_axis=0, tiled=True
     ).reshape(row_count, key_outer.shape[1])
     matching_targets = (
         jnp.zeros((row_count, returned.shape[1]), jnp.float32).at[flat_req].set(returned)
     )
-    grad_in, grad_out = query_grads(
-        query_crops, matching_targets, distractor_bank, query_inner, query_outer, all_rows
-    )
-    return (grad_in, grad_out)
+    return query_grads(
+        crops_t, forward, lane_totals, pull, matching_targets, query_outer, all_rows
+    )
 
 
 def solution(mesh):

time: 180 us -> 158 us (0.88)
  matrix products: 53.8 us -> 22.2 us
  blocking collectives: 20.3 us -> 0 us
  starting transfers between devices: 9.54 us -> 22.9 us
  Pallas kernels: 50.8 us -> 59.3 us
  local copies, waits for them, and re-layouts: 19.5 us -> 23.8 us
  waiting for transfers between devices: 19.8 us -> 21.7 us
  other arithmetic: 5.16 us -> 6.97 us
    dot_general x4 -> x2, matrix products: 40.1 us -> 8.5 us  [the longest x1 7.67 us: query_forward(): hidden = jnp.dot(crop_rows, w_in, preferred_element_type=jnp.float32)]
    all_to_all x1 -> x0, blocking collectives: 20.3 us -> none  [per_device(): lax.all_to_all(wanted, ('dp', 'crop'), split_axis=0, concat_axis=0, tiled...]
    all_to_all x1, waiting for transfers between devices: 19.8 us -> 6.4 us  [per_device(): lax.all_to_all(outgoing, ('dp', 'crop'), split_axis=0, concat_axis=0, til...]
    pallas_call x0 -> x1, Pallas kernels: none -> 12.1 us  [negatives(): pl.pallas_call(functools.partial(negatives_kernel, chunk), grid=(keys //...]
    all_to_all x0 -> x1, starting transfers between devices: none -> 11.2 us  [per_device(): lax.all_to_all(wanted, ('dp', 'crop'), split_axis=0, concat_axis=0, tiled...]
    all_to_all x1, waiting for transfers between devices: 0.01 us -> 9.95 us  [per_device(): lax.all_to_all(embedded, ('dp', 'crop'), split_axis=0, concat_axis=0, til...]
    all_to_all x0 -> x1, waiting for transfers between devices: none -> 5.32 us  [per_device(): lax.all_to_all(wanted, ('dp', 'crop'), split_axis=0, concat_axis=0, tiled...]
    pallas_call x1, Pallas kernels: 50.8 us -> 47.1 us  [summed_grads(): pl.pallas_call(functools.partial(grads_kernel, tiles), out_shape=(jax.Sha...]
  transfers between devices with their start and end apart: 2 -> 3, of which waited for: 1 -> 3; matrix products, arithmetic and copies ran while one was open for 15% -> 9% of each run, Pallas kernels for 0% -> 8%
where the time goes in v3:
time: 158 us
  Pallas kernels  59.3 us (38%)
  local copies, waits for them, and re-layouts  23.8 us (15%)
  starting transfers between devices  22.9 us (14%)
  matrix products  22.2 us (14%)
  waiting for transfers between devices  21.7 us (14%)
  other arithmetic  6.97 us (4%)
    pallas_call x1, Pallas kernels, summed_grads(): pl.pallas_call(functools.partial(grads_kernel, tiles), out_shape=(jax.Sha...  47.1 us
    pallas_call x1, Pallas kernels, negatives(): pl.pallas_call(functools.partial(negatives_kernel, chunk), grid=(keys //...  12.1 us
    all_to_all x1, starting transfers between devices, per_device(): lax.all_to_all(wanted, ('dp', 'crop'), split_axis=0, concat_axis=0, tiled...  11.2 us
    all_to_all x1, waiting for transfers between devices, per_device(): lax.all_to_all(embedded, ('dp', 'crop'), split_axis=0, concat_axis=0, til...  9.95 us
    unnamed x17, local copies, waits for them, and re-layouts  8.74 us
    dot_general x1, matrix products, query_forward(): hidden = jnp.dot(crop_rows, w_in, preferred_element_type=jnp.float32)  7.67 us
    dot_general x1, matrix products, key_embed(): hidden = jnp.dot(crop_rows, w_in, preferred_element_type=jnp.float32)  7.66 us
    all_to_all x1, waiting for transfers between devices, per_device(): lax.all_to_all(outgoing, ('dp', 'crop'), split_axis=0, concat_axis=0, til...  6.4 us
  transfers between devices with their start and end apart: 3, of which 3 were waited for; matrix products, arithmetic and copies ran while one was open for 9% of the time, Pallas kernels for 8%

profile of v3, /device:TPU:0, one launch (start us, length us, event | category | flops | bytes accessed | tf_op | source)
XLA Modules:
  0.0 157.6 jit_solution(15639033647021853900)
XLA Ops:
  0.6 0.0 copy-start
  0.6 0.8 add_select_fusion
  1.5 0.7 all_to_all.12
  2.2 11.2 %all-to-all-start = ((s32[128,1,4]{2,1,0:T(1,128)}), s32[128,1,4]{2,1,0:T(1,128)S(1)}, u32[]{:S(2)}, u32[]{:S(2)}) async-start(s32[128,1,4]{2,1,0:T(1,128)} %bitcast), calls=%async_computation | async-start | bytes 131072 | tf_op jit(solution)/shard_map/all_to_all | solution.py:330
  13.4 3.9 %copy.16 = bf16[512,2048]{0,1:T(8,128)(2,1)} copy(bf16[512,2048]{1,0:T(8,128)(2,1)} %param.8) | data formatting | bytes 4194304 | tf_op args[0]
  17.3 5.3 %all-to-all-done = s32[128,1,4]{2,1,0:T(1,128)S(1)} async-done(((s32[128,1,4]{2,1,0:T(1,128)}), s32[128,1,4]{2,1,0:T(1,128)S(1)}, u32[]{:S(2)}, u32[]{:S(2)}) %all-to-all-start) | async-done | bytes 2080 | tf_op jit(solution)/shard_map/all_to_all | solution.py:330
  22.7 0.5 broadcast.161
  23.2 0.8 reduce.3
  24.0 0.1 reshape.117
  24.1 0.0 copy-done
  24.1 3.3 %gather_fusion = bf16[512,2048]{1,0:T(8,128)(2,1)} fusion(bf16[512,2048]{1,0:T(8,128)(2,1)S(1)} %copy-done, s32[1024]{0:T(1024)S(1)} %pad_clamp_fusion), kind=kCustom, calls=%fused_computation | custom fusion | bytes 4196352 | tf_op jit(solution)/shard_map/gather | solution.py:332
  27.4 4.1 %reshape.118 = bf16[128,4,2048]{2,1,0:T(4,128)(2,1)} reshape(bf16[512,2048]{1,0:T(8,128)(2,1)} %gather_fusion) | data formatting | bytes 4194304 | tf_op jit(solution)/shard_map/reshape | solution.py:332
  31.6 5.8 %all-to-all-start.1 = ((bf16[128,4,2048]{2,1,0:T(4,128)(2,1)}), bf16[128,4,2048]{2,1,0:T(4,128)(2,1)}, u32[]{:S(2)}, u32[]{:S(2)}) async-start(bf16[128,4,2048]{2,1,0:T(4,128)(2,1)} %reshape.118), calls=%async_computation.1 | async-start | bytes 4194304 | tf_op jit(solution)/shard_map/all_to_all | solution.py:333
  37.4 0.0 copy-start.3
  37.4 7.7 %fusion.15 = (f32[2048]{0:T(1024)S(1)}, f32[2048]{0:T(1024)S(1)}, f32[512,2048]{1,0:T(8,128)S(1)}) fusion(bf16[512,2048]{1,0:T(8,128)(2,1)} %param.8, bf16[2048,2048]{1,0:T(8,128)(2,1)} %param.12), kind=kOutput, calls=%fused_computation.48 | convolution fusion | flops 4298108928 | bytes 14696448 | tf_op jit(solution)/shard_map/dot_general | solution.py:281
  45.0 0.0 copy-start.1
  45.1 1.9 %copy-done.1 = f32[512,2048]{1,0:T(8,128)} copy-done((f32[512,2048]{1,0:T(8,128)}, f32[512,2048]{1,0:T(8,128)S(1)}, u32[]{:S(2)}) %copy-start.1) | copy-done | bytes 4194328
  47.0 0.0 copy-done.3
  47.0 0.8 multiply_reduce_fusion.6
  47.8 0.1 copy.15
  47.9 0.9 broadcast_multiply_fusion.1.q_ref
  48.8 12.1 %shard_map.95 = (f32[512,128]{1,0:T(8,128)}, f32[512,128]{1,0:T(8,128)}) custom-call(f32[512,128]{1,0:T(8,128)} %broadcast_multiply_fusion.1.q_ref, bf16[16384,128]{1,0:T(8,128)(2,1)} %bank_ref.1), custom_call_target="tpu_custom_call" | custom-call | flops 4294967296 | bytes 4194304 | tf_op jit(solution)/shard_map/pallas_call | solution.py:249
  60.9 6.4 %all-to-all-done.1 = bf16[128,4,2048]{2,1,0:T(4,128)(2,1)} async-done(((bf16[128,4,2048]{2,1,0:T(4,128)(2,1)}), bf16[128,4,2048]{2,1,0:T(4,128)(2,1)}, u32[]{:S(2)}, u32[]{:S(2)}) %all-to-all-start.1) | async-done | bytes 2097184 | tf_op jit(solution)/shard_map/all_to_all | solution.py:333
  67.3 4.0 %reshape.119 = bf16[512,2048]{1,0:T(8,128)(2,1)} reshape(bf16[128,4,2048]{2,1,0:T(4,128)(2,1)} %all-to-all-done.1) | data formatting | bytes 4194304 | tf_op jit(solution)/shard_map/reshape | solution.py:341
  71.3 0.0 copy-start.5
  71.3 7.7 %fusion.14 = (f32[2048]{0:T(1024)S(1)}, f32[2048]{0:T(1024)S(1)}, f32[512,2048]{1,0:T(8,128)S(1)}) fusion(bf16[512,2048]{1,0:T(8,128)(2,1)} %reshape.119, bf16[2048,2048]{1,0:T(8,128)(2,1)} %param.14), kind=kOutput, calls=%fused_computation.47 | convolution fusion | flops 4298108928 | bytes 14696448 | tf_op jit(solution)/shard_map/dot_general | solution.py:275
  79.0 0.0 copy-start.6
  79.0 0.0 copy-start.4
  79.0 0.0 copy-done.5
  79.0 0.8 multiply_reduce_fusion.5
  79.8 0.8 broadcast_multiply_fusion
  80.7 5.9 %all-to-all-start.2 = ((f32[128,4,128]{2,1,0:T(4,128)}), f32[128,4,128]{2,1,0:T(4,128)}, u32[]{:S(2)}, u32[]{:S(2)}) async-start(f32[128,4,128]{2,1,0:T(4,128)} %bitcast.3), calls=%async_computation.2 | async-start | bytes 524288 | tf_op jit(solution)/shard_map/all_to_all | solution.py:343
  86.6 0.0 copy-done.6
  86.6 0.1 reduce_sum.106
  86.8 10.0 %all-to-all-done.2 = f32[128,4,128]{2,1,0:T(4,128)} async-done(((f32[128,4,128]{2,1,0:T(4,128)}), f32[128,4,128]{2,1,0:T(4,128)}, u32[]{:S(2)}, u32[]{:S(2)}) %all-to-all-start.2) | async-done | bytes 262176 | tf_op jit(solution)/shard_map/all_to_all | solution.py:343
  96.7 2.2 %scatter_custom_fusion = f32[512,128]{1,0:T(8,128)S(1)} fusion(s32[512]{0:T(512)S(1)} %bitcast.16, f32[512,128]{1,0:T(8,128)} %bitcast.4, f32[]{:T(128)} %constant.38.clone.1), kind=kCustom, calls=%fused_computation.23 | custom fusion | bytes 262656 | tf_op jit(solution)/shard_map/scatter | solution.py:347
  98.9 0.2 multiply_reduce_fusion.4
  99.1 0.0 copy-done.4
  99.1 0.4 multiply_reduce_fusion.3
  99.5 0.3 multiply_convert_fusion.1
  99.9 0.0 copy-start.2
  99.9 3.5 %fusion.13 = (f32[2048]{0:T(1024)S(1)}, f32[2048]{0:T(1024)S(1)}, f32[512,2048]{1,0:T(8,128)S(1)}) fusion(f32[2048]{0:T(1024)S(1)} %get-tuple-element.23, f32[512,2048]{1,0:T(8,128)} %copy-done.1, f32[2048]{0:T(1024)S(1)} %get-tuple-element.22, bf16[512,128]{1,0:T(8,128)(2,1)S(1)} %multiply_convert_fusion.1, bf16[2048,128]{1,0:T(8,128)(2,1)S(1)} %copy-done.3), kind=kOutput, calls=%fused_computation.46 | convolution fusion | flops 275771392 | bytes 9076736 | tf_op jit(solution)/shard_map/dot_general | solution.py:312
  103.4 0.0 copy-done.2
  103.4 1.7 %fusion.4.go_ref = f32[2048,128]{1,0:T(8,128)} fusion(bf16[512,128]{1,0:T(8,128)(2,1)S(1)} %multiply_convert_fusion.1, f32[512,2048]{1,0:T(8,128)S(1)} %copy-done.2, f32[2048]{0:T(1024)S(1)} %get-tuple-element.23, f32[2048]{0:T(1024)S(1)} %get-tuple-element.22), kind=kOutput, calls=%fused_computation.14 | convolution fusion | flops 272629760 | bytes 5390336 | tf_op jit(solution)/shard_map/dot_general | solution.py:309
  105.1 2.5 %multiply_convert_fusion.dh_ref = bf16[512,2048]{1,0:T(8,128)(2,1)} fusion(f32[512,2048]{1,0:T(8,128)S(1)} %get-tuple-element.32, f32[512,2048]{1,0:T(8,128)S(1)} %copy-done.2, f32[2048]{0:T(1024)S(1)} %get-tuple-element.33, f32[2048]{0:T(1024)S(1)} %get-tuple-element.34, f32[2048]{0:T(1024)S(1)} %get-tuple-element.23, f32[2048]{0:T(1024)S(1)} %get-tuple-element.22), kind=kLoop, calls=%fused_computation.2 | loop fusion | flops 7340032 | bytes 10518528 | tf_op jit(solution)/shard_map/convert_element_type | solution.py:319
  107.6 47.1 %shard_map.96 = (f32[16,2048]{1,0:T(8,128)}, f32[16,128]{1,0:T(8,128)}) custom-call(bf16[2048,512]{1,0:T(8,128)(2,1)} %bitcast.14, bf16[512,2048]{1,0:T(8,128)(2,1)} %multiply_convert_fusion.dh_ref, f32[2048,128]{1,0:T(8,128)} %fusion.4.go_ref), custom_call_target="tpu_custom_call" | custom-call | tf_op jit(solution)/shard_map/pallas_call | solution.py:203
  154.8 1.6 copy.19
  156.3 1.3 copy.20
  (8 shorter events, 0.1 us)
Async XLA Ops:
  0.6 23.5 %copy-start = (bf16[512,2048]{1,0:T(8,128)(2,1)S(1)}, bf16[512,2048]{1,0:T(8,128)(2,1)}, u32[]{:S(2)}) copy-start(bf16[512,2048]{1,0:T(8,128)(2,1)} %param.9) | copy-start | bytes 6291460
  2.2 20.4 %all-to-all-start = ((s32[128,1,4]{2,1,0:T(1,128)}), s32[128,1,4]{2,1,0:T(1,128)S(1)}, u32[]{:S(2)}, u32[]{:S(2)}) async-start(s32[128,1,4]{2,1,0:T(1,128)} %bitcast), calls=%async_computation | async-start | bytes 131072 | tf_op jit(solution)/shard_map/all_to_all | solution.py:330
  31.6 35.7 %all-to-all-start.1 = ((bf16[128,4,2048]{2,1,0:T(4,128)(2,1)}), bf16[128,4,2048]{2,1,0:T(4,128)(2,1)}, u32[]{:S(2)}, u32[]{:S(2)}) async-start(bf16[128,4,2048]{2,1,0:T(4,128)(2,1)} %reshape.118), calls=%async_computation.1 | async-start | bytes 4194304 | tf_op jit(solution)/shard_map/all_to_all | solution.py:333
  37.4 9.6 %copy-start.3 = (bf16[2048,128]{1,0:T(8,128)(2,1)S(1)}, bf16[2048,128]{1,0:T(8,128)(2,1)}, u32[]{:S(2)}) copy-start(bf16[2048,128]{1,0:T(8,128)(2,1)} %param.13) | copy-start | bytes 1572868
  45.0 1.9 %copy-start.1 = (f32[512,2048]{1,0:T(8,128)}, f32[512,2048]{1,0:T(8,128)S(1)}, u32[]{:S(2)}) copy-start(f32[512,2048]{1,0:T(8,128)S(1)} %get-tuple-element.26) | copy-start | bytes 12582916
  71.3 7.7 %copy-start.5 = (bf16[2048,128]{1,0:T(8,128)(2,1)S(1)}, bf16[2048,128]{1,0:T(8,128)(2,1)}, u32[]{:S(2)}) copy-start(bf16[2048,128]{1,0:T(8,128)(2,1)} %param.15) | copy-start | bytes 1572868
  79.0 7.6 %copy-start.6 = (f32[512,128]{1,0:T(8,128)S(1)}, f32[512,128]{1,0:T(8,128)}, u32[]{:S(2)}) copy-start(f32[512,128]{1,0:T(8,128)} %get-tuple-element.12) | copy-start | bytes 786436
  79.0 20.2 %copy-start.4 = (f32[512,128]{1,0:T(8,128)S(1)}, f32[512,128]{1,0:T(8,128)}, u32[]{:S(2)}) copy-start(f32[512,128]{1,0:T(8,128)} %get-tuple-element.13) | copy-start | bytes 786436
  80.7 16.0 %all-to-all-start.2 = ((f32[128,4,128]{2,1,0:T(4,128)}), f32[128,4,128]{2,1,0:T(4,128)}, u32[]{:S(2)}, u32[]{:S(2)}) async-start(f32[128,4,128]{2,1,0:T(4,128)} %bitcast.3), calls=%async_computation.2 | async-start | bytes 524288 | tf_op jit(solution)/shard_map/all_to_all | solution.py:343
  99.9 3.5 %copy-start.2 = (f32[512,2048]{1,0:T(8,128)S(1)}, f32[512,2048]{1,0:T(8,128)}, u32[]{:S(2)}) copy-start(f32[512,2048]{1,0:T(8,128)} %copy-done.1) | copy-start | bytes 12582916

commit v4 on v3

--- a/solution.py
+++ b/solution.py
@@ -18,6 +18,8 @@
 CHUNK = 16
 LANES = 128
 TURNS = (("x", 1), ("y", 1), ("z", 1), ("x", 3), ("y", 3), ("z", 3))
+BLOCK = 1024
+WIDE = 4
 AXES = ("x", "y", "z")
 
 
@@ -75,6 +77,17 @@
 PLANS = [plan_of(kind) for kind in range(6)]
 
 
+def order_of(tiles, wide):
+    steps, waiting = [("outer", None)], [tiles, tiles + 1]
+    first = waiting + list(range(tiles))
+    for g in range(tiles // wide):
+        steps.append(("block", g))
+        steps += [("hop", 0, t) for t in waiting]
+        waiting = list(range(g * wide, (g + 1) * wide))
+    steps += [("hop", 0, t) for t in waiting]
+    return steps + [("hop", k, t) for k in range(1, 7) for t in first]
+
+
 def grads_kernel(tiles, xt_ref, dh_ref, go_ref, gi_out, go_out, xp, *rest):
     acc, send, recv = rest[0:7], rest[7:14], rest[14:21]
     send_sem, recv_sem = rest[21], rest[22]
@@ -134,54 +147,46 @@
             copy(0, t, t % 6).start()
 
     def inner(g):
-        right = dh_ref[:, 2 * g * LANES : (2 * g + 2) * LANES]
+        right = dh_ref[:, WIDE * g * LANES : (g + 1) * WIDE * LANES]
 
         def block(far, b):
-            left = xp[pl.ds(pl.multiple_of((far * 4 + b) * 256, 256), 256), :]
+            size = BLOCK // CHUNK
+            first = pl.multiple_of(far * 1024 + b * BLOCK, BLOCK)
+            left = xp[pl.ds(first, BLOCK), :]
             part = jnp.dot(left, right, preferred_element_type=jnp.float32)
-            for h in range(2):
-                half = part[:, h * LANES : (h + 1) * LANES].reshape(16, CHUNK, LANES)
-                where = pl.ds(b * 16, 16)
+            for h in range(WIDE):
+                half = part[:, h * LANES : (h + 1) * LANES].reshape(size, CHUNK, LANES)
+                where = pl.ds(b * size, size)
                 if far == 0:
-                    send[0][2 * g + h, where] = half.astype(jnp.bfloat16)
+                    send[0][WIDE * g + h, where] = half.astype(jnp.bfloat16)
                 else:
-                    acc[0][2 * g + h, where] = half
-
-        @pl.loop(0, 4)
-        def _(b):
-            block(0, b)
-
-        for h in range(2):
-            copy(0, 2 * g + h, (2 * g + h) % 6).start()
-
-        @pl.loop(0, 4)
-        def _(b):
-            block(1, b)
-
-    pairs = slots // 2
-    for g in range(pairs + 1):
-        if g < pairs - 1:
-            inner(g)
-        elif g == pairs - 1:
+                    acc[0][WIDE * g + h, where] = half
+
+        for far in (0, 1):
+            if BLOCK == 1024:
+                block(far, 0)
+            else:
+
+                @pl.loop(0, 1024 // BLOCK)
+                def _(b, far=far):
+                    block(far, b)
+
+            if far == 0:
+                for t in range(WIDE * g, WIDE * (g + 1)):
+                    copy(0, t, t % 6).start()
+
+    for step in order_of(tiles, WIDE):
+        if step[0] == "outer":
             outer()
-        if g >= 1:
-            for h in range(2):
-                t = 2 * (g - 1) + h
-                combine(0, t, t % 6)
-
-    for k in range(1, 6):
-
-        @pl.loop(0, slots // 6)
-        def _(r, k=k):
-            for kind in range(6):
-                combine(k, r * 6 + kind, kind)
-
-    for t in range(slots - 1):
-        if t < tiles:
-            gi_out[:, t * LANES : (t + 1) * LANES] = combine(6, t, t % 6)
+        elif step[0] == "block":
+            inner(step[1])
         else:
-            go_out[...] = combine(6, t, t % 6)
-    combine(6, slots - 1, (slots - 1) % 6)
+            _, k, t = step
+            done = combine(k, t, t % 6)
+            if k == 6 and t < tiles:
+                gi_out[:, t * LANES : (t + 1) * LANES] = done
+            elif k == 6 and t == tiles:
+                go_out[...] = done
 
     for k in range(7):
 
@@ -220,6 +225,77 @@
     )(crops_t, d_hidden, grad_outer)
 
 
+def wanted_kernel(order_ref, out_ref, table, keep_sem, send_sem, recv_sem):
+    at = place()
+    barrier = pltpu.get_barrier_semaphore()
+    others = [device_of({**at, "core": 1 - at["core"]})]
+    for axis in AXES:
+        others += [device_of({**at, axis: mirrored(at[axis], u)}) for u in (1, 2, 3)]
+    for other in others:
+        pl.semaphore_signal(barrier, inc=1, device_id=other, device_id_type=MESH)
+    pl.semaphore_wait(barrier, len(others))
+
+    mine = at["x"] * 32 + at["z"] * 8 + at["y"] * 2 + at["core"]
+    keep = pltpu.make_async_copy(order_ref, table.at[:, mine], keep_sem.at[0])
+    keep.start()
+    keep.wait()
+
+    def swap(phase, first, count, targets, sources=None):
+        copies = []
+        for i, target in enumerate(targets):
+            if sources is None:
+                part = (slice(None), pl.ds(first, count))
+                source, landing = table.at[part], table.at[part]
+            else:
+                source = table.at[sources[i], pl.ds(first, count)]
+                landing = out_ref.at[pl.ds(first, count)]
+            copies.append(
+                pltpu.make_async_remote_copy(
+                    src_ref=source,
+                    dst_ref=landing,
+                    send_sem=send_sem.at[phase, i],
+                    recv_sem=recv_sem.at[phase, i],
+                    device_id=target,
+                    device_id_type=MESH,
+                )
+            )
+        for copy in copies:
+            copy.start()
+        return copies
+
+    def finish(copies):
+        for copy in copies:
+            copy.wait()
+
+    finish(swap(0, mine, 1, others[0:1]))
+    finish(swap(1, mine - mine % 2, 2, others[4:7]))
+    finish(swap(2, mine - mine % 8, 8, others[7:10]))
+    block = at["x"] * 32
+    own = pltpu.make_async_copy(
+        table.at[at["x"], pl.ds(block, 32)], out_ref.at[pl.ds(block, 32)], keep_sem.at[1]
+    )
+    own.start()
+    rows = [mirrored(at["x"], u) for u in (1, 2, 3)]
+    finish(swap(3, block, 32, others[1:4], rows))
+    own.wait()
+
+
+def wanted_rows(shuffle):
+    return pl.pallas_call(
+        wanted_kernel,
+        out_shape=jax.ShapeDtypeStruct((128, 1, LANES), jnp.int32),
+        in_specs=[pl.BlockSpec(memory_space=pltpu.VMEM)],
+        out_specs=pl.BlockSpec(memory_space=pltpu.VMEM),
+        scratch_shapes=[
+            pltpu.VMEM((4, 128, 1, LANES), jnp.int32),
+            pltpu.SemaphoreType.DMA((2,)),
+            pltpu.SemaphoreType.DMA((4, 3)),
+            pltpu.SemaphoreType.DMA((4, 3)),
+        ],
+        compiler_params=pltpu.CompilerParams(collective_id=1, has_side_effects=True),
+    )(shuffle.reshape(4, 1, LANES))
+
+
 def negatives_kernel(chunk, q_ref, bank_ref, total_ref, pull_ref):
     @pl.when(pl.program_id(0) == 0)
     def _():
@@ -326,9 +402,11 @@
     row_count = query_crops.shape[0]
     per_peer = row_count // group_count
     all_rows = float(row_count * group_count)
-    wanted = (shuffle % row_count).reshape(group_count, per_peer)
-    requested = lax.all_to_all(wanted, ("dp", "crop"), split_axis=0, concat_axis=0, tiled=True)
-    flat_req = requested.reshape(-1)
+    lane = (lax.axis_index(("dp", "crop")) % 32) * per_peer
+    requested = lax.dynamic_slice_in_dim(
+        wanted_rows(shuffle).reshape(group_count, LANES), lane, per_peer, axis=1
+    )
+    flat_req = requested.reshape(-1) % row_count
     outgoing = key_crops[flat_req].reshape(group_count, per_peer, key_crops.shape[1])
     incoming = lax.all_to_all(outgoing, ("dp", "crop"), split_axis=0, concat_axis=0, tiled=True)
     forward = query_forward(query_crops, query_inner, query_outer)

time: 158 us -> 151 us (0.956)
  Pallas kernels: 59.3 us -> 71.5 us
  waiting for transfers between devices: 21.7 us -> 11.9 us
  starting transfers between devices: 22.9 us -> 13.3 us
    pallas_call x0 -> x1, Pallas kernels: none -> 19.8 us  [wanted_rows(): pl.pallas_call(wanted_kernel, out_shape=jax.ShapeDtypeStruct((128, 1, LAN...]
    all_to_all x1 -> x0, starting transfers between devices: 11.2 us -> none  [per_device(): lax.all_to_all(wanted, ('dp', 'crop'), split_axis=0, concat_axis=0, tiled...]
    pallas_call x1, Pallas kernels: 47.1 us -> 39.6 us  [summed_grads(): pl.pallas_call(functools.partial(grads_kernel, tiles), out_shape=(jax.Sha...]
    all_to_all x1 -> x0, waiting for transfers between devices: 5.32 us -> none  [per_device(): lax.all_to_all(wanted, ('dp', 'crop'), split_axis=0, concat_axis=0, tiled...]
    all_to_all x1, waiting for transfers between devices: 6.4 us -> 2.47 us  [per_device(): lax.all_to_all(outgoing, ('dp', 'crop'), split_axis=0, concat_axis=0, til...]
  transfers between devices with their start and end apart: 3 -> 2, of which waited for: 3 -> 2; matrix products, arithmetic and copies ran while one was open for 9% -> 10% of each run, Pallas kernels for 8% -> 8%
where the time goes in v4:
time: 151 us; the launch traced here: 150 us
  Pallas kernels  71.5 us (47%)
  local copies, waits for them, and re-layouts  24.4 us (16%)
  matrix products  22.2 us (15%)
  starting transfers between devices  13.3 us (9%)
  waiting for transfers between devices  11.9 us (8%)
  other arithmetic  6.29 us (4%)
    pallas_call x1, Pallas kernels, summed_grads(): pl.pallas_call(functools.partial(grads_kernel, tiles), out_shape=(jax.Sha...  39.6 us
    pallas_call x1, Pallas kernels, wanted_rows(): pl.pallas_call(wanted_kernel, out_shape=jax.ShapeDtypeStruct((128, 1, LAN...  19.8 us
    pallas_call x1, Pallas kernels, negatives(): pl.pallas_call(functools.partial(negatives_kernel, chunk), grid=(keys //...  12.1 us
    all_to_all x1, waiting for transfers between devices, per_device(): lax.all_to_all(embedded, ('dp', 'crop'), split_axis=0, concat_axis=0, til...  9.44 us
    unnamed x17, local copies, waits for them, and re-layouts  9.44 us
    dot_general x1, matrix products, key_embed(): hidden = jnp.dot(crop_rows, w_in, preferred_element_type=jnp.float32)  7.66 us
    dot_general x1, matrix products, query_forward(): hidden = jnp.dot(crop_rows, w_in, preferred_element_type=jnp.float32)  7.66 us
    all_to_all x1, starting transfers between devices, per_device(): lax.all_to_all(embedded, ('dp', 'crop'), split_axis=0, concat_axis=0, til...  7.39 us
  transfers between devices with their start and end apart: 2, of which 2 were waited for; matrix products, arithmetic and copies ran while one was open for 10% of the time, Pallas kernels for 8%

profile of v4, /device:TPU:0, one launch (start us, length us, event | category | flops | bytes accessed | tf_op | source)
XLA Modules:
  0.0 150.5 jit_solution(16784743725194034901)
XLA Ops:
  0.6 0.0 copy-start
  0.7 19.8 %shard_map.95 = s32[128,1,128]{2,1,0:T(1,128)} custom-call(s32[4,1,128]{2,1,0:T(1,128)} %bitcast.19), custom_call_target="tpu_custom_call" | custom-call | tf_op jit(solution)/shard_map/pallas_call | solution.py:284
  20.5 1.1 dynamic-slice_reduce_fusion
  21.6 0.1 reshape.152
  21.7 0.0 copy-done
  21.7 3.3 %gather_fusion = bf16[512,2048]{1,0:T(8,128)(2,1)} fusion(bf16[512,2048]{1,0:T(8,128)(2,1)S(1)} %copy-done, s32[1024]{0:T(1024)S(1)} %pad_clamp_fusion), kind=kCustom, calls=%fused_computation | custom fusion | bytes 4196352 | tf_op jit(solution)/shard_map/gather | solution.py:410
  25.1 4.1 %reshape.153 = bf16[128,4,2048]{2,1,0:T(4,128)(2,1)} reshape(bf16[512,2048]{1,0:T(8,128)(2,1)} %gather_fusion) | data formatting | bytes 4194304 | tf_op jit(solution)/shard_map/reshape | solution.py:410
  29.2 5.9 %all-to-all-start = ((bf16[128,4,2048]{2,1,0:T(4,128)(2,1)}), bf16[128,4,2048]{2,1,0:T(4,128)(2,1)}, u32[]{:S(2)}, u32[]{:S(2)}) async-start(bf16[128,4,2048]{2,1,0:T(4,128)(2,1)} %reshape.153), calls=%async_computation | async-start | bytes 4194304 | tf_op jit(solution)/shard_map/all_to_all | solution.py:411
  35.2 3.9 %copy.13 = bf16[512,2048]{0,1:T(8,128)(2,1)} copy(bf16[512,2048]{1,0:T(8,128)(2,1)} %param.8) | data formatting | bytes 4194304 | tf_op args[0]
  39.1 0.0 copy-start.3
  39.1 7.7 %fusion.15 = (f32[2048]{0:T(1024)S(1)}, f32[2048]{0:T(1024)S(1)}, f32[512,2048]{1,0:T(8,128)S(1)}) fusion(bf16[512,2048]{1,0:T(8,128)(2,1)} %param.8, bf16[2048,2048]{1,0:T(8,128)(2,1)} %param.12), kind=kOutput, calls=%fused_computation.49 | convolution fusion | flops 4298108928 | bytes 14696448 | tf_op jit(solution)/shard_map/dot_general | solution.py:357
  46.8 0.0 copy-start.1
  46.8 1.9 %copy-done.1 = f32[512,2048]{1,0:T(8,128)} copy-done((f32[512,2048]{1,0:T(8,128)}, f32[512,2048]{1,0:T(8,128)S(1)}, u32[]{:S(2)}) %copy-start.1) | copy-done | bytes 4194328
  48.7 0.0 copy-done.3
  48.7 0.8 multiply_reduce_fusion.6
  49.5 0.1 copy.12
  49.7 0.9 broadcast_multiply_fusion.1.q_ref
  50.5 12.1 %shard_map.96 = (f32[512,128]{1,0:T(8,128)}, f32[512,128]{1,0:T(8,128)}) custom-call(f32[512,128]{1,0:T(8,128)} %broadcast_multiply_fusion.1.q_ref, bf16[16384,128]{1,0:T(8,128)(2,1)} %bank_ref.1), custom_call_target="tpu_custom_call" | custom-call | flops 4294967296 | bytes 4194304 | tf_op jit(solution)/shard_map/pallas_call | solution.py:325
  62.6 2.5 %all-to-all-done = bf16[128,4,2048]{2,1,0:T(4,128)(2,1)} async-done(((bf16[128,4,2048]{2,1,0:T(4,128)(2,1)}), bf16[128,4,2048]{2,1,0:T(4,128)(2,1)}, u32[]{:S(2)}, u32[]{:S(2)}) %all-to-all-start) | async-done | bytes 2097184 | tf_op jit(solution)/shard_map/all_to_all | solution.py:411
  65.1 4.0 %reshape.154 = bf16[512,2048]{1,0:T(8,128)(2,1)} reshape(bf16[128,4,2048]{2,1,0:T(4,128)(2,1)} %all-to-all-done) | data formatting | bytes 4194304 | tf_op jit(solution)/shard_map/reshape | solution.py:419
  69.1 0.0 copy-start.5
  69.1 7.7 %fusion.14 = (f32[2048]{0:T(1024)S(1)}, f32[2048]{0:T(1024)S(1)}, f32[512,2048]{1,0:T(8,128)S(1)}) fusion(bf16[512,2048]{1,0:T(8,128)(2,1)} %reshape.154, bf16[2048,2048]{1,0:T(8,128)(2,1)} %param.14), kind=kOutput, calls=%fused_computation.48 | convolution fusion | flops 4298108928 | bytes 14696448 | tf_op jit(solution)/shard_map/dot_general | solution.py:351
  76.8 0.0 copy-start.4
  76.8 0.0 copy-done.5
  76.8 0.8 multiply_reduce_fusion.5
  77.6 0.9 broadcast_multiply_fusion
  78.5 7.4 %all-to-all-start.1 = ((f32[128,4,128]{2,1,0:T(4,128)}), f32[128,4,128]{2,1,0:T(4,128)S(1)}, u32[]{:S(2)}, u32[]{:S(2)}) async-start(f32[128,4,128]{2,1,0:T(4,128)} %bitcast.15), calls=%async_computation.1 | async-start | bytes 524288 | tf_op jit(solution)/shard_map/all_to_all | solution.py:421
  85.9 1.1 reduce_sum.106
  87.0 9.4 %all-to-all-done.1 = f32[128,4,128]{2,1,0:T(4,128)S(1)} async-done(((f32[128,4,128]{2,1,0:T(4,128)}), f32[128,4,128]{2,1,0:T(4,128)S(1)}, u32[]{:S(2)}, u32[]{:S(2)}) %all-to-all-start.1) | async-done | bytes 262176 | tf_op jit(solution)/shard_map/all_to_all | solution.py:421
  96.4 0.0 copy-start.6
  96.4 0.7 copy-done.6
  97.1 2.2 %scatter_custom_fusion = f32[512,128]{1,0:T(8,128)S(1)} fusion(s32[512]{0:T(512)S(1)} %bitcast.18, f32[512,128]{1,0:T(8,128)} %bitcast.16, f32[]{:T(128)} %constant.65.clone.1), kind=kCustom, calls=%fused_computation.23 | custom fusion | bytes 262656 | tf_op jit(solution)/shard_map/scatter | solution.py:425
  99.3 0.2 multiply_reduce_fusion.4
  99.6 0.0 copy-done.4
  99.6 0.4 multiply_reduce_fusion.3
  99.9 0.3 multiply_convert_fusion.1
  100.3 0.0 copy-start.2
  100.3 3.5 %fusion.13 = (f32[2048]{0:T(1024)S(1)}, f32[2048]{0:T(1024)S(1)}, f32[512,2048]{1,0:T(8,128)S(1)}) fusion(f32[2048]{0:T(1024)S(1)} %get-tuple-element.23, f32[512,2048]{1,0:T(8,128)} %copy-done.1, f32[2048]{0:T(1024)S(1)} %get-tuple-element.22, bf16[512,128]{1,0:T(8,128)(2,1)S(1)} %multiply_convert_fusion.1, bf16[2048,128]{1,0:T(8,128)(2,1)S(1)} %copy-done.3), kind=kOutput, calls=%fused_computation.47 | convolution fusion | flops 275771392 | bytes 9076736 | tf_op jit(solution)/shard_map/dot_general | solution.py:388
  103.8 0.0 copy-done.2
  103.8 1.7 %fusion.4.go_ref = f32[2048,128]{1,0:T(8,128)} fusion(bf16[512,128]{1,0:T(8,128)(2,1)S(1)} %multiply_convert_fusion.1, f32[512,2048]{1,0:T(8,128)S(1)} %copy-done.2, f32[2048]{0:T(1024)S(1)} %get-tuple-element.23, f32[2048]{0:T(1024)S(1)} %get-tuple-element.22), kind=kOutput, calls=%fused_computation.14 | convolution fusion | flops 272629760 | bytes 5390336 | tf_op jit(solution)/shard_map/dot_general | solution.py:385
  105.6 2.5 %multiply_convert_fusion.dh_ref = bf16[512,2048]{1,0:T(8,128)(2,1)} fusion(f32[512,2048]{1,0:T(8,128)S(1)} %get-tuple-element.32, f32[512,2048]{1,0:T(8,128)S(1)} %copy-done.2, f32[2048]{0:T(1024)S(1)} %get-tuple-element.33, f32[2048]{0:T(1024)S(1)} %get-tuple-element.34, f32[2048]{0:T(1024)S(1)} %get-tuple-element.23, f32[2048]{0:T(1024)S(1)} %get-tuple-element.22), kind=kLoop, calls=%fused_computation.2 | loop fusion | flops 7340032 | bytes 10518528 | tf_op jit(solution)/shard_map/convert_element_type | solution.py:395
  108.0 39.6 %shard_map.97 = (f32[16,2048]{1,0:T(8,128)}, f32[16,128]{1,0:T(8,128)}) custom-call(bf16[2048,512]{1,0:T(8,128)(2,1)} %bitcast.14, bf16[512,2048]{1,0:T(8,128)(2,1)} %multiply_convert_fusion.dh_ref, f32[2048,128]{1,0:T(8,128)} %fusion.4.go_ref), custom_call_target="tpu_custom_call" | custom-call | tf_op jit(solution)/shard_map/pallas_call | solution.py:208
  147.6 1.6 %copy.16 = f32[16,2048]{1,0:T(8,128)} copy(f32[16,2048]{1,0:T(8,128)} %get-tuple-element.37) | data formatting | bytes 262144
  149.2 1.3 copy.17
  (8 shorter events, 0.1 us)
Async XLA Ops:
  0.6 21.1 %copy-start = (bf16[512,2048]{1,0:T(8,128)(2,1)S(1)}, bf16[512,2048]{1,0:T(8,128)(2,1)}, u32[]{:S(2)}) copy-start(bf16[512,2048]{1,0:T(8,128)(2,1)} %param.9) | copy-start | bytes 6291460
  29.2 35.9 %all-to-all-start = ((bf16[128,4,2048]{2,1,0:T(4,128)(2,1)}), bf16[128,4,2048]{2,1,0:T(4,128)(2,1)}, u32[]{:S(2)}, u32[]{:S(2)}) async-start(bf16[128,4,2048]{2,1,0:T(4,128)(2,1)} %reshape.153), calls=%async_computation | async-start | bytes 4194304 | tf_op jit(solution)/shard_map/all_to_all | solution.py:411
  39.1 9.6 %copy-start.3 = (bf16[2048,128]{1,0:T(8,128)(2,1)S(1)}, bf16[2048,128]{1,0:T(8,128)(2,1)}, u32[]{:S(2)}) copy-start(bf16[2048,128]{1,0:T(8,128)(2,1)} %param.13) | copy-start | bytes 1572868
  46.8 1.9 %copy-start.1 = (f32[512,2048]{1,0:T(8,128)}, f32[512,2048]{1,0:T(8,128)S(1)}, u32[]{:S(2)}) copy-start(f32[512,2048]{1,0:T(8,128)S(1)} %get-tuple-element.26) | copy-start | bytes 12582916
  69.1 7.7 %copy-start.5 = (bf16[2048,128]{1,0:T(8,128)(2,1)S(1)}, bf16[2048,128]{1,0:T(8,128)(2,1)}, u32[]{:S(2)}) copy-start(bf16[2048,128]{1,0:T(8,128)(2,1)} %param.15) | copy-start | bytes 1572868
  76.8 22.8 %copy-start.4 = (f32[512,128]{1,0:T(8,128)S(1)}, f32[512,128]{1,0:T(8,128)}, u32[]{:S(2)}) copy-start(f32[512,128]{1,0:T(8,128)} %get-tuple-element.13) | copy-start | bytes 786436
  78.5 17.9 %all-to-all-start.1 = ((f32[128,4,128]{2,1,0:T(4,128)}), f32[128,4,128]{2,1,0:T(4,128)S(1)}, u32[]{:S(2)}, u32[]{:S(2)}) async-start(f32[128,4,128]{2,1,0:T(4,128)} %bitcast.15), calls=%async_computation.1 | async-start | bytes 524288 | tf_op jit(solution)/shard_map/all_to_all | solution.py:421
  96.4 0.7 copy-start.6
  100.3 3.5 %copy-start.2 = (f32[512,2048]{1,0:T(8,128)S(1)}, f32[512,2048]{1,0:T(8,128)}, u32[]{:S(2)}) copy-start(f32[512,2048]{1,0:T(8,128)} %copy-done.1) | copy-start | bytes 12582916

commit v5 on v4

--- a/solution.py
+++ b/solution.py
@@ -46,13 +46,6 @@
         return device_of({**at, "core": 1 - at["core"]})
     axis, flip = turn
     return device_of({**at, axis: mirrored(at[axis], flip)})
-
-
-def greet(at):
-    barrier = pltpu.get_barrier_semaphore()
-    for turn in (None,) + TURNS:
-        pl.semaphore_signal(barrier, inc=1, device_id=partner(at, turn), device_id_type=MESH)
-    pl.semaphore_wait(barrier, 1 + len(TURNS))
 
 
 def plan_of(kind):
@@ -88,12 +81,16 @@
     return steps + [("hop", k, t) for k in range(1, 7) for t in first]
 
 
-def grads_kernel(tiles, xt_ref, dh_ref, go_ref, gi_out, go_out, xp, *rest):
+def grads_kernel(
+    tiles, xt_ref, hid_ref, stats_ref, dz_ref, w_ref, go_ref, out_ref, xp, slope, *rest
+):
     acc, send, recv = rest[0:7], rest[7:14], rest[14:21]
     send_sem, recv_sem = rest[21], rest[22]
     slots = tiles + 2
     at = place()
-    greet(at)
+    barrier = pltpu.get_barrier_semaphore()
+    for turn in (None,) + TURNS:
+        pl.semaphore_signal(barrier, inc=1, device_id=partner(at, turn), device_id_type=MESH)
 
     def copy(k, t, kind):
         turn = None if k == 0 else TURNS[(kind + k - 1) % 6]
@@ -143,11 +140,22 @@
             acc[0][tiles, i] = go_ref[pl.ds(rows[64 + i], CHUNK), :]
         send[0][tiles + 1] = jnp.zeros((64, CHUNK, LANES), jnp.bfloat16)
         acc[0][tiles + 1] = jnp.zeros((64, CHUNK, LANES), jnp.float32)
+        pl.semaphore_wait(barrier, 1 + len(TURNS))
         for t in (tiles, tiles + 1):
             copy(0, t, t % 6).start()
 
     def inner(g):
-        right = dh_ref[:, WIDE * g * LANES : (g + 1) * WIDE * LANES]
+        cols = slice(WIDE * g * LANES, (g + 1) * WIDE * LANES)
+        inv_std = stats_ref[1:2, cols]
+        normed = (hid_ref[:, cols] - stats_ref[0:1, cols]) * inv_std
+        d_act = lax.dot_general(
+            dz_ref[...], w_ref[cols, :], (((1,), (1,)), ((), ())), preferred_element_type=jnp.float32
+        )
+        d_norm = jnp.where(normed > 0.0, d_act, 0.0)
+        d_mean = jnp.mean(d_norm, axis=0, keepdims=True)
+        d_pull = jnp.mean(d_norm * normed, axis=0, keepdims=True)
+        slope[g % 2] = (inv_std * (d_norm - d_mean - normed * d_pull)).astype(jnp.bfloat16)
+        right = slope[g % 2]
 
         def block(far, b):
             size = BLOCK // CHUNK
@@ -183,10 +191,8 @@
         else:
             _, k, t = step
             done = combine(k, t, t % 6)
-            if k == 6 and t < tiles:
-                gi_out[:, t * LANES : (t + 1) * LANES] = done
-            elif k == 6 and t == tiles:
-                go_out[...] = done
+            if k == 6 and t <= tiles:
+                out_ref[:, t * LANES : (t + 1) * LANES] = done
 
     for k in range(7):
 
@@ -196,33 +202,33 @@
                 copy(k, r * 6 + kind, kind).wait_send()
 
 
-def summed_grads(crops_t, d_hidden, grad_outer):
+def summed_grads(crops_t, hidden, stats, d_proj, w_out, grad_outer):
     depth, batch = crops_t.shape
-    width = d_hidden.shape[1]
+    width = hidden.shape[1]
     tiles = width // LANES
     slots = tiles + 2
 
     def slabs(dtype):
         return [pltpu.VMEM((slots, 64 >> k, CHUNK, LANES), dtype) for k in range(7)]
 
-    return pl.pallas_call(
+    summed = pl.pallas_call(
         functools.partial(grads_kernel, tiles),
-        out_shape=(
-            jax.ShapeDtypeStruct((CHUNK, width), jnp.float32),
-            jax.ShapeDtypeStruct((CHUNK, LANES), jnp.float32),
-        ),
-        in_specs=[pl.BlockSpec(memory_space=pltpu.VMEM)] * 3,
-        out_specs=[pl.BlockSpec(memory_space=pltpu.VMEM)] * 2,
-        scratch_shapes=[pltpu.VMEM((depth, batch), jnp.bfloat16)]
+        out_shape=jax.ShapeDtypeStruct((CHUNK, width + LANES), jnp.float32),
+        in_specs=[pl.BlockSpec(memory_space=pltpu.VMEM)] * 6,
+        out_specs=pl.BlockSpec(memory_space=pltpu.VMEM),
+        scratch_shapes=[
+            pltpu.VMEM((depth, batch), jnp.bfloat16),
+            pltpu.VMEM((2, batch, WIDE * LANES), jnp.bfloat16),
+        ]
         + slabs(jnp.float32)
-        + [pltpu.VMEM((slots, 64, CHUNK, LANES), jnp.bfloat16)]
-        + slabs(jnp.bfloat16)[1:]
+        + slabs(jnp.bfloat16)
         + slabs(jnp.bfloat16)
         + [pltpu.SemaphoreType.DMA((7, slots)), pltpu.SemaphoreType.DMA((7, slots))],
         compiler_params=pltpu.CompilerParams(
-            collective_id=0, has_side_effects=True, vmem_limit_bytes=60 << 20
+            collective_id=0, has_side_effects=True, vmem_limit_bytes=56 << 20
         ),
-    )(crops_t, d_hidden, grad_outer)
+    )(crops_t, hidden, stats, d_proj, w_out, grad_outer)
+    return (summed[:, :width], summed[:, width:])
 
 
 def wanted_kernel(order_ref, out_ref, table, keep_sem, send_sem, recv_sem):
@@ -331,7 +337,7 @@
         cost_estimate=pl.CostEstimate(
             flops=4 * rows * keys * emb, bytes_accessed=2 * keys * emb, transcendentals=rows * keys
         ),
-        compiler_params=pltpu.CompilerParams(vmem_limit_bytes=60 << 20),
+        compiler_params=pltpu.CompilerParams(vmem_limit_bytes=24 << 20),
     )(probe_features, distractor_bank)
 
 
@@ -343,14 +349,15 @@
 
 def head_tail(normed, w_out):
     active = jnp.maximum(normed, 0.0).astype(jnp.bfloat16)
-    projected = jnp.dot(active, w_out, preferred_element_type=jnp.float32)
+    projected = jnp.einsum("gjh,he->gje", active, w_out, preferred_element_type=jnp.float32)
     return projected * lax.rsqrt(jnp.sum(projected * projected, axis=-1, keepdims=True) + norm_eps)
 
 
 def key_embed(crop_rows, w_in, w_out):
-    hidden = jnp.dot(crop_rows, w_in, preferred_element_type=jnp.float32)
-    average, inv_std = batch_stats(hidden)
-    return head_tail((hidden - average) * inv_std, w_out)
+    hidden = jnp.einsum("gjd,dh->gjh", crop_rows, w_in, preferred_element_type=jnp.float32)
+    average = jnp.mean(hidden, axis=(0, 1))
+    variance = jnp.mean(hidden * hidden, axis=(0, 1)) - average * average
+    return head_tail((hidden - average) * lax.rsqrt(variance + bn_eps), w_out)
 
 
 def query_forward(crop_rows, w_in, w_out):
@@ -360,11 +367,12 @@
     active = jnp.maximum(normed, 0.0).astype(jnp.bfloat16)
     projected = jnp.dot(active, w_out, preferred_element_type=jnp.float32)
     inv_len = lax.rsqrt(jnp.sum(projected * projected, axis=-1, keepdims=True) + norm_eps)
-    return (normed, active, inv_std, inv_len, projected * inv_len)
+    stats = jnp.stack([average, inv_std])
+    return (hidden, stats, active, inv_len, projected * inv_len)
 
 
 def query_grads(crops_t, forward, lane_totals, pull, matching_targets, w_out, all_rows):
-    normed, active, inv_std, inv_len, probe_features = forward
+    hidden, stats, active, inv_len, probe_features = forward
     matching_similarity = (
         jnp.sum(probe_features * matching_targets, axis=-1, keepdims=True) / sharpness_divisor
     )
@@ -385,14 +393,7 @@
     grad_out = lax.dot_general(
         active, d_proj, (((0,), (0,)), ((), ())), preferred_element_type=jnp.float32
     )
-    d_act = lax.dot_general(
-        d_proj, w_out, (((1,), (1,)), ((), ())), preferred_element_type=jnp.float32
-    )
-    d_norm = jnp.where(normed > 0.0, d_act, 0.0)
-    d_hidden = inv_std * (
-        d_norm - jnp.mean(d_norm, axis=0) - normed * jnp.mean(d_norm * normed, axis=0)
-    )
-    return summed_grads(crops_t, d_hidden.astype(jnp.bfloat16), grad_out)
+    return summed_grads(crops_t, hidden, stats, d_proj, w_out, grad_out)
 
 
 def per_device(
@@ -415,9 +416,7 @@
     incoming, lane_totals, pull, crops_t = lax.optimization_barrier(
         (incoming, lane_totals, pull, crops_t)
     )
-    embedded = key_embed(
-        incoming.reshape(row_count, key_crops.shape[1]), key_inner, key_outer
-    ).reshape(group_count, per_peer, key_outer.shape[1])
+    embedded = key_embed(incoming, key_inner, key_outer)
     returned = lax.all_to_all(
         embedded, ("dp", "crop"), split_axis=0, concat_axis=0, tiled=True
     ).reshape(row_count, key_outer.shape[1])

time: 151 us -> 146 us (0.967)
  other arithmetic: 6.29 us -> 1.96 us
  local copies, waits for them, and re-layouts: 24.4 us -> 22.5 us
  matrix products: 22.2 us -> 23.9 us
    reshape x1 -> x0, local copies, waits for them, and re-layouts: 3.99 us -> none  [per_device(): incoming.reshape(row_count, key_crops.shape[1])]
    slice x0 -> x2, local copies, waits for them, and re-layouts: none -> 2.86 us  [summed_grads(): return (summed[:, :width], summed[:, width:])]
    convert_element_type x1 -> x0, other arithmetic: 2.47 us -> none  [query_grads(): return summed_grads(crops_t, d_hidden.astype(jnp.bfloat16), grad_out)]
    dot_general x1, matrix products: 1.74 us -> 3.99 us  [query_grads(): lax.dot_general(active, d_proj, (((0,), (0,)), ((), ())), preferred_eleme...]
    pallas_call x1, Pallas kernels: 12.1 us -> 10.1 us  [negatives(): pl.pallas_call(functools.partial(negatives_kernel, chunk), grid=(keys //...]
    unnamed x17 -> x13, local copies, waits for them, and re-layouts: 9.44 us -> 8.05 us
    dot_general x3 -> x2, matrix products: 12 us -> 11.4 us  [the longest x1 10.6 us: key_embed(): jnp.einsum('gjd,dh->gjh', crop_rows, w_in, preferred_element_type=jnp.flo...]
  transfers between devices with their start and end apart: 2 -> 2, of which waited for: 2 -> 2; matrix products, arithmetic and copies ran while one was open for 10% -> 9% of each run, Pallas kernels for 8% -> 7%
where the time goes in v5:
time: 146 us
  Pallas kernels  70.9 us (49%)
  matrix products  23.9 us (16%)
  local copies, waits for them, and re-layouts  22.5 us (15%)
  starting transfers between devices  12.9 us (9%)
  waiting for transfers between devices  12.7 us (9%)
  other arithmetic  1.96 us (1%)
    pallas_call x1, Pallas kernels, summed_grads(): pl.pallas_call(functools.partial(grads_kernel, tiles), out_shape=jax.Shap...  41 us
    pallas_call x1, Pallas kernels, wanted_rows(): pl.pallas_call(wanted_kernel, out_shape=jax.ShapeDtypeStruct((128, 1, LAN...  19.8 us
    dot_general x1, matrix products, key_embed(): jnp.einsum('gjd,dh->gjh', crop_rows, w_in, preferred_element_type=jnp.flo...  10.6 us
    pallas_call x1, Pallas kernels, negatives(): pl.pallas_call(functools.partial(negatives_kernel, chunk), grid=(keys //...  10.1 us
    all_to_all x1, waiting for transfers between devices, per_device(): lax.all_to_all(embedded, ('dp', 'crop'), split_axis=0, concat_axis=0, til...  9.93 us
    unnamed x13, local copies, waits for them, and re-layouts  8.05 us
    dot_general x1, matrix products, query_forward(): hidden = jnp.dot(crop_rows, w_in, preferred_element_type=jnp.float32)  7.66 us
    all_to_all x1, starting transfers between devices, per_device(): lax.all_to_all(embedded, ('dp', 'crop'), split_axis=0, concat_axis=0, til...  6.78 us
  transfers between devices with their start and end apart: 2, of which 2 were waited for; matrix products, arithmetic and copies ran while one was open for 9% of the time, Pallas kernels for 7%

profile of v5, /device:TPU:0, one launch (start us, length us, event | category | flops | bytes accessed | tf_op | source)
XLA Modules:
  0.0 145.7 jit_solution(7845986898860798615)
XLA Ops:
  0.6 0.0 copy-start
  0.7 19.8 %shard_map.95 = s32[128,1,128]{2,1,0:T(1,128)} custom-call(s32[4,1,128]{2,1,0:T(1,128)} %bitcast.28), custom_call_target="tpu_custom_call" | custom-call | tf_op jit(solution)/shard_map/pallas_call | solution.py:290
  20.5 1.1 dynamic-slice_reduce_fusion
  21.6 0.1 reshape.162
  21.7 0.0 copy-done
  21.7 3.3 %gather_fusion = bf16[512,2048]{1,0:T(8,128)(2,1)} fusion(bf16[512,2048]{1,0:T(8,128)(2,1)S(1)} %copy-done, s32[1024]{0:T(1024)S(1)} %pad_clamp_fusion), kind=kCustom, calls=%fused_computation | custom fusion | bytes 4196352 | tf_op jit(solution)/shard_map/gather | solution.py:411
  25.1 4.1 %reshape.163 = bf16[128,4,2048]{2,1,0:T(4,128)(2,1)} reshape(bf16[512,2048]{1,0:T(8,128)(2,1)} %gather_fusion) | data formatting | bytes 4194304 | tf_op jit(solution)/shard_map/reshape | solution.py:411
  29.2 6.1 %all-to-all-start = ((bf16[128,4,2048]{2,1,0:T(4,128)(2,1)}), bf16[128,4,2048]{2,1,0:T(4,128)(2,1)}, u32[]{:S(2)}, u32[]{:S(2)}) async-start(bf16[128,4,2048]{2,1,0:T(4,128)(2,1)} %reshape.163), calls=%async_computation | async-start | bytes 4194304 | tf_op jit(solution)/shard_map/all_to_all | solution.py:412
  35.3 3.9 %copy.21 = bf16[512,2048]{0,1:T(8,128)(2,1)} copy(bf16[512,2048]{1,0:T(8,128)(2,1)} %param.8) | data formatting | bytes 4194304 | tf_op args[0]
  39.3 0.0 copy-start.3
  39.3 7.7 %multiply_reduce_fusion.1 = (f32[2048]{0:T(1024)S(1)}, f32[2048]{0:T(1024)S(1)}, f32[512,2048]{1,0:T(8,128)S(1)}) fusion(bf16[512,2048]{1,0:T(8,128)(2,1)} %param.8, bf16[2048,2048]{1,0:T(8,128)(2,1)} %param.12), kind=kOutput, calls=%fused_computation.7 | convolution fusion | flops 4298108928 | bytes 14696448 | tf_op jit(solution)/shard_map/dot_general | solution.py:364
  46.9 0.0 copy-start.2
  47.0 1.9 %copy-done.2 = f32[512,2048]{1,0:T(8,128)} copy-done((f32[512,2048]{1,0:T(8,128)}, f32[512,2048]{1,0:T(8,128)S(1)}, u32[]{:S(2)}) %copy-start.2) | copy-done | bytes 4194328
  48.9 0.0 copy-done.3
  48.9 0.8 multiply_reduce_fusion.5
  49.7 0.1 copy.20
  49.8 0.1 broadcast_multiply_fusion.1.q_ref
  50.0 0.0 copy-start.1
  50.0 2.2 %copy-done.1 = bf16[16384,128]{1,0:T(8,128)(2,1)S(1)} copy-done((bf16[16384,128]{1,0:T(8,128)(2,1)S(1)}, bf16[16384,128]{1,0:T(8,128)(2,1)}, u32[]{:S(2)}) %copy-start.1) | copy-done | bytes 4194328
  52.2 10.1 %shard_map.96 = (f32[512,128]{1,0:T(8,128)S(1)}, f32[512,128]{1,0:T(8,128)S(1)}) custom-call(f32[512,128]{1,0:T(8,128)S(1)} %broadcast_multiply_fusion.1.q_ref, bf16[16384,128]{1,0:T(8,128)(2,1)S(1)} %copy-done.1), custom_call_target="tpu_custom_call" | custom-call | flops 4294967296 | bytes 4194304 | tf_op jit(solution)/shard_map/pallas_call | solution.py:331
  62.3 2.8 %all-to-all-done = bf16[128,4,2048]{2,1,0:T(4,128)(2,1)} async-done(((bf16[128,4,2048]{2,1,0:T(4,128)(2,1)}), bf16[128,4,2048]{2,1,0:T(4,128)(2,1)}, u32[]{:S(2)}, u32[]{:S(2)}) %all-to-all-start) | async-done | bytes 2097184 | tf_op jit(solution)/shard_map/all_to_all | solution.py:412
  65.1 0.0 copy-start.5
  65.1 10.6 %fusion.17 = (f32[2048]{0:T(1024)S(1)}, f32[2048]{0:T(1024)S(1)}, f32[128,4,2048]{2,0,1:T(8,128)S(1)}) fusion(bf16[2048,2048]{1,0:T(8,128)(2,1)} %param.14, bf16[128,4,2048]{2,1,0:T(4,128)(2,1)} %all-to-all-done), kind=kOutput, calls=%fused_computation.48 | convolution fusion | flops 4298108928 | bytes 14696448 | tf_op jit(solution)/shard_map/gjd,dh->gjh/dot_general | solution.py:357
  75.7 0.0 copy-done.5
  75.7 0.8 multiply_reduce_fusion.4
  76.6 0.8 copy.24
  77.4 6.8 %all-to-all-start.1 = ((f32[128,4,128]{2,1,0:T(4,128)}), f32[128,4,128]{2,1,0:T(4,128)S(1)}, u32[]{:S(2)}, u32[]{:S(2)}) async-start(f32[128,4,128]{2,1,0:T(4,128)} %copy.24), calls=%async_computation.1 | async-start | bytes 524288 | tf_op jit(solution)/shard_map/all_to_all | solution.py:420
  84.2 0.6 pad_maximum_fusion.stats_ref
  84.8 0.1 reduce_sum.88
  85.0 9.9 %all-to-all-done.1 = f32[128,4,128]{2,1,0:T(4,128)S(1)} async-done(((f32[128,4,128]{2,1,0:T(4,128)}), f32[128,4,128]{2,1,0:T(4,128)S(1)}, u32[]{:S(2)}, u32[]{:S(2)}) %all-to-all-start.1) | async-done | bytes 262176 | tf_op jit(solution)/shard_map/all_to_all | solution.py:420
  94.9 2.0 %scatter_custom_fusion = f32[512,128]{1,0:T(8,128)S(1)} fusion(s32[512]{0:T(512)S(1)} %bitcast.27, f32[512,128]{1,0:T(8,128)S(1)} %bitcast.22, f32[]{:T(128)} %constant.65.clone.1), kind=kCustom, calls=%fused_computation.23 | custom fusion | bytes 262148 | tf_op jit(solution)/shard_map/scatter | solution.py:424
  96.9 0.2 multiply_reduce_fusion.3
  97.2 0.4 multiply_reduce_fusion.2
  97.6 0.3 multiply_convert_fusion.dz_ref
  97.9 0.0 copy-start.4
  97.9 4.0 %fusion.8.go_ref = f32[2048,128]{1,0:T(8,128)} fusion(bf16[512,128]{1,0:T(8,128)(2,1)S(1)} %multiply_convert_fusion.dz_ref, f32[512,2048]{1,0:T(8,128)} %copy-done.2, f32[2048]{0:T(1024)S(1)} %get-tuple-element.21, f32[2048]{0:T(1024)S(1)} %get-tuple-element.22), kind=kOutput, calls=%fused_computation.14 | convolution fusion | flops 272629760 | bytes 5390336 | tf_op jit(solution)/shard_map/dot_general | solution.py:393
  101.9 0.0 copy-done.4
  101.9 41.0 %shard_map.97 = f32[16,2176]{1,0:T(8,128)} custom-call(bf16[2048,512]{1,0:T(8,128)(2,1)} %bitcast.21, f32[512,2048]{1,0:T(8,128)} %copy-done.2, f32[2,2048]{1,0:T(2,128)} %pad_maximum_fusion.stats_ref, bf16[512,128]{1,0:T(8,128)(2,1)} %copy-done.4, bf16[2048,128]{1,0:T(8,128)(2,1)} %w_ref.1, f32[2048,128]{1,0:T(8,128)} %fusion.8.go_ref), custom_call_target="tpu_custom_call" | custom-call | tf_op jit(solution)/shard_map/pallas_call | solution.py:214
  142.9 1.3 slice.7
  144.2 1.6 %slice.6 = f32[16,2048]{1,0:T(8,128)} slice(f32[16,2176]{1,0:T(8,128)} %shard_map.97), slice={[0:16], [0:2048]} | slice | bytes 262144 | tf_op jit(solution)/shard_map/slice | solution.py:231
  (9 shorter events, 0.1 us)
Async XLA Ops:
  0.6 21.1 %copy-start = (bf16[512,2048]{1,0:T(8,128)(2,1)S(1)}, bf16[512,2048]{1,0:T(8,128)(2,1)}, u32[]{:S(2)}) copy-start(bf16[512,2048]{1,0:T(8,128)(2,1)} %param.9) | copy-start | bytes 6291460
  29.2 35.9 %all-to-all-start = ((bf16[128,4,2048]{2,1,0:T(4,128)(2,1)}), bf16[128,4,2048]{2,1,0:T(4,128)(2,1)}, u32[]{:S(2)}, u32[]{:S(2)}) async-start(bf16[128,4,2048]{2,1,0:T(4,128)(2,1)} %reshape.163), calls=%async_computation | async-start | bytes 4194304 | tf_op jit(solution)/shard_map/all_to_all | solution.py:412
  39.3 9.6 %copy-start.3 = (bf16[2048,128]{1,0:T(8,128)(2,1)S(1)}, bf16[2048,128]{1,0:T(8,128)(2,1)}, u32[]{:S(2)}) copy-start(bf16[2048,128]{1,0:T(8,128)(2,1)} %w_ref.1) | copy-start | bytes 1572868
  46.9 1.9 %copy-start.2 = (f32[512,2048]{1,0:T(8,128)}, f32[512,2048]{1,0:T(8,128)S(1)}, u32[]{:S(2)}) copy-start(f32[512,2048]{1,0:T(8,128)S(1)} %get-tuple-element.25.hid_ref) | copy-start | bytes 12582916
  50.0 2.2 %copy-start.1 = (bf16[16384,128]{1,0:T(8,128)(2,1)S(1)}, bf16[16384,128]{1,0:T(8,128)(2,1)}, u32[]{:S(2)}) copy-start(bf16[16384,128]{1,0:T(8,128)(2,1)} %bank_ref.1) | copy-start | bytes 12582916
  65.1 10.6 %copy-start.5 = (bf16[2048,128]{1,0:T(8,128)(2,1)S(1)}, bf16[2048,128]{1,0:T(8,128)(2,1)}, u32[]{:S(2)}) copy-start(bf16[2048,128]{1,0:T(8,128)(2,1)} %param.15) | copy-start | bytes 1572868
  77.4 17.5 %all-to-all-start.1 = ((f32[128,4,128]{2,1,0:T(4,128)}), f32[128,4,128]{2,1,0:T(4,128)S(1)}, u32[]{:S(2)}, u32[]{:S(2)}) async-start(f32[128,4,128]{2,1,0:T(4,128)} %copy.24), calls=%async_computation.1 | async-start | bytes 524288 | tf_op jit(solution)/shard_map/all_to_all | solution.py:420
  97.9 4.0 %copy-start.4 = (bf16[512,128]{1,0:T(8,128)(2,1)}, bf16[512,128]{1,0:T(8,128)(2,1)S(1)}, u32[]{:S(2)}) copy-start(bf16[512,128]{1,0:T(8,128)(2,1)S(1)} %multiply_convert_fusion.dz_ref) | copy-start | bytes 393220

commit v6 on v5

--- a/solution.py
+++ b/solution.py
@@ -71,18 +71,32 @@
 
 
 def order_of(tiles, wide):
-    steps, waiting = [("outer", None)], [tiles, tiles + 1]
-    first = waiting + list(range(tiles))
+    steps, waiting = [], []
+    first = list(range(tiles + 2))
     for g in range(tiles // wide):
         steps.append(("block", g))
         steps += [("hop", 0, t) for t in waiting]
-        waiting = list(range(g * wide, (g + 1) * wide))
-    steps += [("hop", 0, t) for t in waiting]
+        waiting = first[g * wide : (g + 1) * wide]
+    steps.append(("outer", None))
+    steps += [("hop", 0, t) for t in waiting + first[tiles:]]
     return steps + [("hop", k, t) for k in range(1, 7) for t in first]
 
 
 def grads_kernel(
-    tiles, xt_ref, hid_ref, stats_ref, dz_ref, w_ref, go_ref, out_ref, xp, slope, *rest
+    tiles,
+    xt_any,
+    hid_any,
+    stats_ref,
+    dz_ref,
+    w_ref,
+    out_ref,
+    xt_ref,
+    hid_ref,
+    go_ref,
+    load_sem,
+    xp,
+    slope,
+    *rest,
 ):
     acc, send, recv = rest[0:7], rest[7:14], rest[14:21]
     send_sem, recv_sem = rest[21], rest[22]
@@ -91,6 +105,19 @@
     barrier = pltpu.get_barrier_semaphore()
     for turn in (None,) + TURNS:
         pl.semaphore_signal(barrier, inc=1, device_id=partner(at, turn), device_id_type=MESH)
+
+    def columns(g):
+        return slice(WIDE * g * LANES, (g + 1) * WIDE * LANES)
+
+    blocks = tiles // WIDE
+    loads = [
+        pltpu.make_async_copy(hid_any.at[:, columns(g)], hid_ref.at[g], load_sem.at[g])
+        for g in range(blocks)
+    ]
+    loads.append(pltpu.make_async_copy(xt_any, xt_ref, load_sem.at[blocks]))
+    for i in (blocks, *range(blocks)):
+        loads[i].start()
+    loads[blocks].wait()
 
     def copy(k, t, kind):
         turn = None if k == 0 else TURNS[(kind + k - 1) % 6]
@@ -140,14 +167,14 @@
             acc[0][tiles, i] = go_ref[pl.ds(rows[64 + i], CHUNK), :]
         send[0][tiles + 1] = jnp.zeros((64, CHUNK, LANES), jnp.bfloat16)
         acc[0][tiles + 1] = jnp.zeros((64, CHUNK, LANES), jnp.float32)
-        pl.semaphore_wait(barrier, 1 + len(TURNS))
         for t in (tiles, tiles + 1):
             copy(0, t, t % 6).start()
 
     def inner(g):
-        cols = slice(WIDE * g * LANES, (g + 1) * WIDE * LANES)
+        cols = columns(g)
+        loads[g].wait()
         inv_std = stats_ref[1:2, cols]
-        normed = (hid_ref[:, cols] - stats_ref[0:1, cols]) * inv_std
+        normed = (hid_ref[g] - stats_ref[0:1, cols]) * inv_std
         d_act = lax.dot_general(
             dz_ref[...], w_ref[cols, :], (((1,), (1,)), ((), ())), preferred_element_type=jnp.float32
         )
@@ -180,8 +207,16 @@
                     block(far, b)
 
             if far == 0:
+                if g == 0:
+                    pl.semaphore_wait(barrier, 1 + len(TURNS))
                 for t in range(WIDE * g, WIDE * (g + 1)):
                     copy(0, t, t % 6).start()
+
+        active = jnp.maximum(normed, 0.0).astype(jnp.bfloat16)
+        turned = lax.dot_general(
+            dz_ref[...], active, (((0,), (0,)), ((), ())), preferred_element_type=jnp.float32
+        )
+        go_ref[cols, :] = jnp.transpose(turned)
 
     for step in order_of(tiles, WIDE):
         if step[0] == "outer":
@@ -202,7 +237,7 @@
                 copy(k, r * 6 + kind, kind).wait_send()
 
 
-def summed_grads(crops_t, hidden, stats, d_proj, w_out, grad_outer):
+def summed_grads(crops_t, hidden, stats, d_proj, w_out):
     depth, batch = crops_t.shape
     width = hidden.shape[1]
     tiles = width // LANES
@@ -214,9 +249,14 @@
     summed = pl.pallas_call(
         functools.partial(grads_kernel, tiles),
         out_shape=jax.ShapeDtypeStruct((CHUNK, width + LANES), jnp.float32),
-        in_specs=[pl.BlockSpec(memory_space=pltpu.VMEM)] * 6,
+        in_specs=[pl.BlockSpec(memory_space=pl.ANY)] * 2
+        + [pl.BlockSpec(memory_space=pltpu.VMEM)] * 3,
         out_specs=pl.BlockSpec(memory_space=pltpu.VMEM),
         scratch_shapes=[
+            pltpu.VMEM((depth, batch), jnp.bfloat16),
+            pltpu.VMEM((tiles // WIDE, batch, WIDE * LANES), jnp.float32),
+            pltpu.VMEM((width, LANES), jnp.float32),
+            pltpu.SemaphoreType.DMA((tiles // WIDE + 1,)),
             pltpu.VMEM((depth, batch), jnp.bfloat16),
             pltpu.VMEM((2, batch, WIDE * LANES), jnp.bfloat16),
         ]
@@ -227,7 +267,7 @@
         compiler_params=pltpu.CompilerParams(
             collective_id=0, has_side_effects=True, vmem_limit_bytes=56 << 20
         ),
-    )(crops_t, hidden, stats, d_proj, w_out, grad_outer)
+    )(crops_t, hidden, stats, d_proj, w_out)
     return (summed[:, :width], summed[:, width:])
 
 
@@ -368,11 +408,11 @@
     projected = jnp.dot(active, w_out, preferred_element_type=jnp.float32)
     inv_len = lax.rsqrt(jnp.sum(projected * projected, axis=-1, keepdims=True) + norm_eps)
     stats = jnp.stack([average, inv_std])
-    return (hidden, stats, active, inv_len, projected * inv_len)
+    return (hidden, stats, inv_len, projected * inv_len)
 
 
 def query_grads(crops_t, forward, lane_totals, pull, matching_targets, w_out, all_rows):
-    hidden, stats, active, inv_len, probe_features = forward
+    hidden, stats, inv_len, probe_features = forward
     matching_similarity = (
         jnp.sum(probe_features * matching_targets, axis=-1, keepdims=True) / sharpness_divisor
     )
@@ -390,10 +430,7 @@
         )
         * inv_len
     ).astype(jnp.bfloat16)
-    grad_out = lax.dot_general(
-        active, d_proj, (((0,), (0,)), ((), ())), preferred_element_type=jnp.float32
-    )
-    return summed_grads(crops_t, hidden, stats, d_proj, w_out, grad_out)
+    return summed_grads(crops_t, hidden, stats, d_proj, w_out)
 
 
 def per_device(
@@ -412,7 +449,7 @@
     incoming = lax.all_to_all(outgoing, ("dp", "crop"), split_axis=0, concat_axis=0, tiled=True)
     forward = query_forward(query_crops, query_inner, query_outer)
     crops_t = query_crops.T
-    lane_totals, pull = negatives(forward[4], distractor_bank)
+    lane_totals, pull = negatives(forward[3], distractor_bank)
     incoming, lane_totals, pull, crops_t = lax.optimization_barrier(
         (incoming, lane_totals, pull, crops_t)
     )

time: 146 us -> 142 us (0.973)
  matrix products: 23.9 us -> 19.9 us
    dot_general x1 -> x0, matrix products: 3.99 us -> none  [query_grads(): lax.dot_general(active, d_proj, (((0,), (0,)), ((), ())), preferred_eleme...]
    unnamed x13 -> x11, local copies, waits for them, and re-layouts: 8.05 us -> 8.04 us
  transfers between devices with their start and end apart: 2 -> 2, of which waited for: 2 -> 2; matrix products, arithmetic and copies ran while one was open for 9% -> 10% of each run, Pallas kernels for 7% -> 7%
where the time goes in v6:
time: 142 us
  Pallas kernels  70.2 us (49%)
  local copies, waits for them, and re-layouts  22.5 us (16%)
  matrix products  19.9 us (14%)
  starting transfers between devices  12.9 us (9%)
  waiting for transfers between devices  12.7 us (9%)
  other arithmetic  2.62 us (2%)
    pallas_call x1, Pallas kernels, summed_grads(): pl.pallas_call(functools.partial(grads_kernel, tiles), out_shape=jax.Shap...  40.3 us
    pallas_call x1, Pallas kernels, wanted_rows(): pl.pallas_call(wanted_kernel, out_shape=jax.ShapeDtypeStruct((128, 1, LAN...  19.8 us
    dot_general x1, matrix products, key_embed(): jnp.einsum('gjd,dh->gjh', crop_rows, w_in, preferred_element_type=jnp.flo...  10.6 us
    pallas_call x1, Pallas kernels, negatives(): pl.pallas_call(functools.partial(negatives_kernel, chunk), grid=(keys //...  10.1 us
    all_to_all x1, waiting for transfers between devices, per_device(): lax.all_to_all(embedded, ('dp', 'crop'), split_axis=0, concat_axis=0, til...  9.93 us
    unnamed x11, local copies, waits for them, and re-layouts  8.04 us
    dot_general x1, matrix products, query_forward(): hidden = jnp.dot(crop_rows, w_in, preferred_element_type=jnp.float32)  7.66 us
    all_to_all x1, starting transfers between devices, per_device(): lax.all_to_all(embedded, ('dp', 'crop'), split_axis=0, concat_axis=0, til...  6.75 us
  transfers between devices with their start and end apart: 2, of which 2 were waited for; matrix products, arithmetic and copies ran while one was open for 10% of the time, Pallas kernels for 7%

profile of v6, /device:TPU:0, one launch (start us, length us, event | category | flops | bytes accessed | tf_op | source)
XLA Modules:
  0.0 141.7 jit_solution(10570122963352294359)
XLA Ops:
  0.6 0.0 copy-start
  0.7 19.8 %shard_map.95 = s32[128,1,128]{2,1,0:T(1,128)} custom-call(s32[4,1,128]{2,1,0:T(1,128)} %bitcast.27), custom_call_target="tpu_custom_call" | custom-call | tf_op jit(solution)/shard_map/pallas_call | solution.py:330
  20.5 1.1 dynamic-slice_reduce_fusion
  21.6 0.1 reshape.162
  21.7 0.0 copy-done
  21.7 3.3 %gather_fusion = bf16[512,2048]{1,0:T(8,128)(2,1)} fusion(bf16[512,2048]{1,0:T(8,128)(2,1)S(1)} %copy-done, s32[1024]{0:T(1024)S(1)} %pad_clamp_fusion), kind=kCustom, calls=%fused_computation | custom fusion | bytes 4196352 | tf_op jit(solution)/shard_map/gather | solution.py:448
  25.1 4.1 %reshape.163 = bf16[128,4,2048]{2,1,0:T(4,128)(2,1)} reshape(bf16[512,2048]{1,0:T(8,128)(2,1)} %gather_fusion) | data formatting | bytes 4194304 | tf_op jit(solution)/shard_map/reshape | solution.py:448
  29.2 6.1 %all-to-all-start = ((bf16[128,4,2048]{2,1,0:T(4,128)(2,1)}), bf16[128,4,2048]{2,1,0:T(4,128)(2,1)}, u32[]{:S(2)}, u32[]{:S(2)}) async-start(bf16[128,4,2048]{2,1,0:T(4,128)(2,1)} %reshape.163), calls=%async_computation | async-start | bytes 4194304 | tf_op jit(solution)/shard_map/all_to_all | solution.py:449
  35.3 3.9 %copy.21 = bf16[512,2048]{0,1:T(8,128)(2,1)} copy(bf16[512,2048]{1,0:T(8,128)(2,1)} %param.8) | data formatting | bytes 4194304 | tf_op args[0]
  39.3 0.0 copy-start.3
  39.3 7.7 %multiply_reduce_fusion.1 = (f32[2048]{0:T(1024)S(1)}, f32[2048]{0:T(1024)S(1)}, f32[512,2048]{1,0:T(8,128)S(1)}) fusion(bf16[512,2048]{1,0:T(8,128)(2,1)} %param.8, bf16[2048,2048]{1,0:T(8,128)(2,1)} %param.12), kind=kOutput, calls=%fused_computation.7 | convolution fusion | flops 4298108928 | bytes 14696448 | tf_op jit(solution)/shard_map/dot_general | solution.py:404
  46.9 0.0 copy-start.2
  47.0 1.9 %copy-done.2 = f32[512,2048]{1,0:T(8,128)} copy-done((f32[512,2048]{1,0:T(8,128)}, f32[512,2048]{1,0:T(8,128)S(1)}, u32[]{:S(2)}) %copy-start.2) | copy-done | bytes 4194328
  48.9 0.0 copy-done.3
  48.9 0.8 multiply_reduce_fusion.5
  49.7 0.1 copy.20
  49.8 0.1 broadcast_multiply_fusion.1.q_ref
  50.0 0.0 copy-start.1
  50.0 2.2 %copy-done.1 = bf16[16384,128]{1,0:T(8,128)(2,1)S(1)} copy-done((bf16[16384,128]{1,0:T(8,128)(2,1)S(1)}, bf16[16384,128]{1,0:T(8,128)(2,1)}, u32[]{:S(2)}) %copy-start.1) | copy-done | bytes 4194328
  52.2 10.1 %shard_map.96 = (f32[512,128]{1,0:T(8,128)S(1)}, f32[512,128]{1,0:T(8,128)S(1)}) custom-call(f32[512,128]{1,0:T(8,128)S(1)} %broadcast_multiply_fusion.1.q_ref, bf16[16384,128]{1,0:T(8,128)(2,1)S(1)} %copy-done.1), custom_call_target="tpu_custom_call" | custom-call | flops 4294967296 | bytes 4194304 | tf_op jit(solution)/shard_map/pallas_call | solution.py:371
  62.3 2.8 %all-to-all-done = bf16[128,4,2048]{2,1,0:T(4,128)(2,1)} async-done(((bf16[128,4,2048]{2,1,0:T(4,128)(2,1)}), bf16[128,4,2048]{2,1,0:T(4,128)(2,1)}, u32[]{:S(2)}, u32[]{:S(2)}) %all-to-all-start) | async-done | bytes 2097184 | tf_op jit(solution)/shard_map/all_to_all | solution.py:449
  65.1 0.0 copy-start.4
  65.1 10.6 %fusion.18 = (f32[2048]{0:T(1024)S(1)}, f32[2048]{0:T(1024)S(1)}, f32[128,4,2048]{2,0,1:T(8,128)S(1)}) fusion(bf16[2048,2048]{1,0:T(8,128)(2,1)} %param.14, bf16[128,4,2048]{2,1,0:T(4,128)(2,1)} %all-to-all-done), kind=kOutput, calls=%fused_computation.49 | convolution fusion | flops 4298108928 | bytes 14696448 | tf_op jit(solution)/shard_map/gjd,dh->gjh/dot_general | solution.py:397
  75.7 0.0 copy-done.4
  75.7 0.8 multiply_reduce_fusion.4
  76.6 0.8 copy.24
  77.4 6.7 %all-to-all-start.1 = ((f32[128,4,128]{2,1,0:T(4,128)}), f32[128,4,128]{2,1,0:T(4,128)S(1)}, u32[]{:S(2)}, u32[]{:S(2)}) async-start(f32[128,4,128]{2,1,0:T(4,128)} %copy.24), calls=%async_computation.1 | async-start | bytes 524288 | tf_op jit(solution)/shard_map/all_to_all | solution.py:457
  84.2 0.6 pad_maximum_fusion.stats_ref
  84.8 0.1 reduce_sum.88
  85.0 9.9 %all-to-all-done.1 = f32[128,4,128]{2,1,0:T(4,128)S(1)} async-done(((f32[128,4,128]{2,1,0:T(4,128)}), f32[128,4,128]{2,1,0:T(4,128)S(1)}, u32[]{:S(2)}, u32[]{:S(2)}) %all-to-all-start.1) | async-done | bytes 262176 | tf_op jit(solution)/shard_map/all_to_all | solution.py:457
  94.9 2.0 %scatter_custom_fusion = f32[512,128]{1,0:T(8,128)S(1)} fusion(s32[512]{0:T(512)S(1)} %bitcast.26, f32[512,128]{1,0:T(8,128)S(1)} %bitcast.21, f32[]{:T(128)} %constant.65.clone.1), kind=kCustom, calls=%fused_computation.25 | custom fusion | bytes 262148 | tf_op jit(solution)/shard_map/scatter | solution.py:461
  96.9 0.2 multiply_reduce_fusion.3
  97.1 0.4 multiply_reduce_fusion.2
  97.5 1.0 multiply_convert_fusion.dz_ref
  98.5 40.3 %shard_map.97 = f32[16,2176]{1,0:T(8,128)} custom-call(bf16[2048,512]{1,0:T(8,128)(2,1)} %bitcast.20, f32[512,2048]{1,0:T(8,128)} %copy-done.2, f32[2,2048]{1,0:T(2,128)} %pad_maximum_fusion.stats_ref, bf16[512,128]{1,0:T(8,128)(2,1)} %multiply_convert_fusion.dz_ref, bf16[2048,128]{1,0:T(8,128)(2,1)} %w_ref.1), custom_call_target="tpu_custom_call" | custom-call | tf_op jit(solution)/shard_map/pallas_call | solution.py:249
  138.8 1.3 slice.7
  140.1 1.6 %slice.6 = f32[16,2048]{1,0:T(8,128)} slice(f32[16,2176]{1,0:T(8,128)} %shard_map.97), slice={[0:16], [0:2048]} | slice | bytes 262144 | tf_op jit(solution)/shard_map/slice | solution.py:271
  (9 shorter events, 0.1 us)
Async XLA Ops:
  0.6 21.1 %copy-start = (bf16[512,2048]{1,0:T(8,128)(2,1)S(1)}, bf16[512,2048]{1,0:T(8,128)(2,1)}, u32[]{:S(2)}) copy-start(bf16[512,2048]{1,0:T(8,128)(2,1)} %param.9) | copy-start | bytes 6291460
  29.2 35.9 %all-to-all-start = ((bf16[128,4,2048]{2,1,0:T(4,128)(2,1)}), bf16[128,4,2048]{2,1,0:T(4,128)(2,1)}, u32[]{:S(2)}, u32[]{:S(2)}) async-start(bf16[128,4,2048]{2,1,0:T(4,128)(2,1)} %reshape.163), calls=%async_computation | async-start | bytes 4194304 | tf_op jit(solution)/shard_map/all_to_all | solution.py:449
  39.3 9.6 %copy-start.3 = (bf16[2048,128]{1,0:T(8,128)(2,1)S(1)}, bf16[2048,128]{1,0:T(8,128)(2,1)}, u32[]{:S(2)}) copy-start(bf16[2048,128]{1,0:T(8,128)(2,1)} %w_ref.1) | copy-start | bytes 1572868
  46.9 1.9 %copy-start.2 = (f32[512,2048]{1,0:T(8,128)}, f32[512,2048]{1,0:T(8,128)S(1)}, u32[]{:S(2)}) copy-start(f32[512,2048]{1,0:T(8,128)S(1)} %get-tuple-element.25.hid_any) | copy-start | bytes 12582916
  50.0 2.2 %copy-start.1 = (bf16[16384,128]{1,0:T(8,128)(2,1)S(1)}, bf16[16384,128]{1,0:T(8,128)(2,1)}, u32[]{:S(2)}) copy-start(bf16[16384,128]{1,0:T(8,128)(2,1)} %bank_ref.1) | copy-start | bytes 12582916
  65.1 10.6 %copy-start.4 = (bf16[2048,128]{1,0:T(8,128)(2,1)S(1)}, bf16[2048,128]{1,0:T(8,128)(2,1)}, u32[]{:S(2)}) copy-start(bf16[2048,128]{1,0:T(8,128)(2,1)} %param.15) | copy-start | bytes 1572868
  77.4 17.5 %all-to-all-start.1 = ((f32[128,4,128]{2,1,0:T(4,128)}), f32[128,4,128]{2,1,0:T(4,128)S(1)}, u32[]{:S(2)}, u32[]{:S(2)}) async-start(f32[128,4,128]{2,1,0:T(4,128)} %copy.24), calls=%async_computation.1 | async-start | bytes 524288 | tf_op jit(solution)/shard_map/all_to_all | solution.py:457

commit v7 on v6

--- a/solution.py
+++ b/solution.py
@@ -284,7 +284,6 @@
     mine = at["x"] * 32 + at["z"] * 8 + at["y"] * 2 + at["core"]
     keep = pltpu.make_async_copy(order_ref, table.at[:, mine], keep_sem.at[0])
     keep.start()
-    keep.wait()
 
     def swap(phase, first, count, targets, sources=None):
         copies = []
@@ -313,7 +312,17 @@
         for copy in copies:
             copy.wait()
 
-    finish(swap(0, mine, 1, others[0:1]))
+    first = pltpu.make_async_remote_copy(
+        src_ref=order_ref,
+        dst_ref=table.at[:, mine],
+        send_sem=send_sem.at[0, 0],
+        recv_sem=recv_sem.at[0, 0],
+        device_id=others[0],
+        device_id_type=MESH,
+    )
+    first.start()
+    keep.wait()
+    first.wait()
     finish(swap(1, mine - mine % 2, 2, others[4:7]))
     finish(swap(2, mine - mine % 8, 8, others[7:10]))
     block = at["x"] * 32

time: 142 us -> 142 us (level)
  no operation moved by 1% of the time
where the time goes in v7:
time: 142 us
  Pallas kernels  70.2 us (49%)
  local copies, waits for them, and re-layouts  22.5 us (16%)
  matrix products  19.9 us (14%)
  starting transfers between devices  12.9 us (9%)
  waiting for transfers between devices  12.7 us (9%)
  other arithmetic  2.62 us (2%)
    pallas_call x1, Pallas kernels, summed_grads(): pl.pallas_call(functools.partial(grads_kernel, tiles), out_shape=jax.Shap...  40.3 us
    pallas_call x1, Pallas kernels, wanted_rows(): pl.pallas_call(wanted_kernel, out_shape=jax.ShapeDtypeStruct((128, 1, LAN...  19.8 us
    dot_general x1, matrix products, key_embed(): jnp.einsum('gjd,dh->gjh', crop_rows, w_in, preferred_element_type=jnp.flo...  10.6 us
    pallas_call x1, Pallas kernels, negatives(): pl.pallas_call(functools.partial(negatives_kernel, chunk), grid=(keys //...  10.1 us
    all_to_all x1, waiting for transfers between devices, per_device(): lax.all_to_all(embedded, ('dp', 'crop'), split_axis=0, concat_axis=0, til...  9.93 us
    unnamed x11, local copies, waits for them, and re-layouts  8.04 us
    dot_general x1, matrix products, query_forward(): hidden = jnp.dot(crop_rows, w_in, preferred_element_type=jnp.float32)  7.66 us
    all_to_all x1, starting transfers between devices, per_device(): lax.all_to_all(embedded, ('dp', 'crop'), split_axis=0, concat_axis=0, til...  6.78 us
  transfers between devices with their start and end apart: 2, of which 2 were waited for; matrix products, arithmetic and copies ran while one was open for 10% of the time, Pallas kernels for 7%

profile of v7, /device:TPU:0, one launch (start us, length us, event | category | flops | bytes accessed | tf_op | source)
XLA Modules:
  0.0 141.7 jit_solution(9689327563505833289)
XLA Ops:
  0.6 0.0 copy-start
  0.7 19.8 %shard_map.95 = s32[128,1,128]{2,1,0:T(1,128)} custom-call(s32[4,1,128]{2,1,0:T(1,128)} %bitcast.27), custom_call_target="tpu_custom_call" | custom-call | tf_op jit(solution)/shard_map/pallas_call | solution.py:339
  20.5 1.1 dynamic-slice_reduce_fusion
  21.6 0.1 reshape.162
  21.7 0.0 copy-done
  21.7 3.3 %gather_fusion = bf16[512,2048]{1,0:T(8,128)(2,1)} fusion(bf16[512,2048]{1,0:T(8,128)(2,1)S(1)} %copy-done, s32[1024]{0:T(1024)S(1)} %pad_clamp_fusion), kind=kCustom, calls=%fused_computation | custom fusion | bytes 4196352 | tf_op jit(solution)/shard_map/gather | solution.py:457
  25.1 4.1 %reshape.163 = bf16[128,4,2048]{2,1,0:T(4,128)(2,1)} reshape(bf16[512,2048]{1,0:T(8,128)(2,1)} %gather_fusion) | data formatting | bytes 4194304 | tf_op jit(solution)/shard_map/reshape | solution.py:457
  29.2 6.1 %all-to-all-start = ((bf16[128,4,2048]{2,1,0:T(4,128)(2,1)}), bf16[128,4,2048]{2,1,0:T(4,128)(2,1)}, u32[]{:S(2)}, u32[]{:S(2)}) async-start(bf16[128,4,2048]{2,1,0:T(4,128)(2,1)} %reshape.163), calls=%async_computation | async-start | bytes 4194304 | tf_op jit(solution)/shard_map/all_to_all | solution.py:458
  35.3 3.9 %copy.21 = bf16[512,2048]{0,1:T(8,128)(2,1)} copy(bf16[512,2048]{1,0:T(8,128)(2,1)} %param.8) | data formatting | bytes 4194304 | tf_op args[0]
  39.3 0.0 copy-start.3
  39.3 7.7 %multiply_reduce_fusion.1 = (f32[2048]{0:T(1024)S(1)}, f32[2048]{0:T(1024)S(1)}, f32[512,2048]{1,0:T(8,128)S(1)}) fusion(bf16[512,2048]{1,0:T(8,128)(2,1)} %param.8, bf16[2048,2048]{1,0:T(8,128)(2,1)} %param.12), kind=kOutput, calls=%fused_computation.7 | convolution fusion | flops 4298108928 | bytes 14696448 | tf_op jit(solution)/shard_map/dot_general | solution.py:413
  46.9 0.0 copy-start.2
  47.0 1.9 %copy-done.2 = f32[512,2048]{1,0:T(8,128)} copy-done((f32[512,2048]{1,0:T(8,128)}, f32[512,2048]{1,0:T(8,128)S(1)}, u32[]{:S(2)}) %copy-start.2) | copy-done | bytes 4194328
  48.9 0.0 copy-done.3
  48.9 0.8 multiply_reduce_fusion.5
  49.7 0.1 copy.20
  49.8 0.1 broadcast_multiply_fusion.1.q_ref
  50.0 0.0 copy-start.1
  50.0 2.2 %copy-done.1 = bf16[16384,128]{1,0:T(8,128)(2,1)S(1)} copy-done((bf16[16384,128]{1,0:T(8,128)(2,1)S(1)}, bf16[16384,128]{1,0:T(8,128)(2,1)}, u32[]{:S(2)}) %copy-start.1) | copy-done | bytes 4194328
  52.2 10.1 %shard_map.96 = (f32[512,128]{1,0:T(8,128)S(1)}, f32[512,128]{1,0:T(8,128)S(1)}) custom-call(f32[512,128]{1,0:T(8,128)S(1)} %broadcast_multiply_fusion.1.q_ref, bf16[16384,128]{1,0:T(8,128)(2,1)S(1)} %copy-done.1), custom_call_target="tpu_custom_call" | custom-call | flops 4294967296 | bytes 4194304 | tf_op jit(solution)/shard_map/pallas_call | solution.py:380
  62.3 2.8 %all-to-all-done = bf16[128,4,2048]{2,1,0:T(4,128)(2,1)} async-done(((bf16[128,4,2048]{2,1,0:T(4,128)(2,1)}), bf16[128,4,2048]{2,1,0:T(4,128)(2,1)}, u32[]{:S(2)}, u32[]{:S(2)}) %all-to-all-start) | async-done | bytes 2097184 | tf_op jit(solution)/shard_map/all_to_all | solution.py:458
  65.1 0.0 copy-start.4
  65.1 10.6 %fusion.18 = (f32[2048]{0:T(1024)S(1)}, f32[2048]{0:T(1024)S(1)}, f32[128,4,2048]{2,0,1:T(8,128)S(1)}) fusion(bf16[2048,2048]{1,0:T(8,128)(2,1)} %param.14, bf16[128,4,2048]{2,1,0:T(4,128)(2,1)} %all-to-all-done), kind=kOutput, calls=%fused_computation.49 | convolution fusion | flops 4298108928 | bytes 14696448 | tf_op jit(solution)/shard_map/gjd,dh->gjh/dot_general | solution.py:406
  75.7 0.0 copy-done.4
  75.7 0.8 multiply_reduce_fusion.4
  76.6 0.8 copy.24
  77.4 6.8 %all-to-all-start.1 = ((f32[128,4,128]{2,1,0:T(4,128)}), f32[128,4,128]{2,1,0:T(4,128)S(1)}, u32[]{:S(2)}, u32[]{:S(2)}) async-start(f32[128,4,128]{2,1,0:T(4,128)} %copy.24), calls=%async_computation.1 | async-start | bytes 524288 | tf_op jit(solution)/shard_map/all_to_all | solution.py:466
  84.2 0.6 pad_maximum_fusion.stats_ref
  84.8 0.1 reduce_sum.88
  85.0 9.9 %all-to-all-done.1 = f32[128,4,128]{2,1,0:T(4,128)S(1)} async-done(((f32[128,4,128]{2,1,0:T(4,128)}), f32[128,4,128]{2,1,0:T(4,128)S(1)}, u32[]{:S(2)}, u32[]{:S(2)}) %all-to-all-start.1) | async-done | bytes 262176 | tf_op jit(solution)/shard_map/all_to_all | solution.py:466
  94.9 2.0 %scatter_custom_fusion = f32[512,128]{1,0:T(8,128)S(1)} fusion(s32[512]{0:T(512)S(1)} %bitcast.26, f32[512,128]{1,0:T(8,128)S(1)} %bitcast.21, f32[]{:T(128)} %constant.65.clone.1), kind=kCustom, calls=%fused_computation.25 | custom fusion | bytes 262148 | tf_op jit(solution)/shard_map/scatter | solution.py:470
  96.9 0.2 multiply_reduce_fusion.3
  97.2 0.4 multiply_reduce_fusion.2
  97.6 1.0 multiply_convert_fusion.dz_ref
  98.6 40.3 %shard_map.97 = f32[16,2176]{1,0:T(8,128)} custom-call(bf16[2048,512]{1,0:T(8,128)(2,1)} %bitcast.20, f32[512,2048]{1,0:T(8,128)} %copy-done.2, f32[2,2048]{1,0:T(2,128)} %pad_maximum_fusion.stats_ref, bf16[512,128]{1,0:T(8,128)(2,1)} %multiply_convert_fusion.dz_ref, bf16[2048,128]{1,0:T(8,128)(2,1)} %w_ref.1), custom_call_target="tpu_custom_call" | custom-call | tf_op jit(solution)/shard_map/pallas_call | solution.py:249
  138.9 1.3 slice.7
  140.2 1.6 %slice.6 = f32[16,2048]{1,0:T(8,128)} slice(f32[16,2176]{1,0:T(8,128)} %shard_map.97), slice={[0:16], [0:2048]} | slice | bytes 262144 | tf_op jit(solution)/shard_map/slice | solution.py:271
  (9 shorter events, 0.1 us)
Async XLA Ops:
  0.6 21.1 %copy-start = (bf16[512,2048]{1,0:T(8,128)(2,1)S(1)}, bf16[512,2048]{1,0:T(8,128)(2,1)}, u32[]{:S(2)}) copy-start(bf16[512,2048]{1,0:T(8,128)(2,1)} %param.9) | copy-start | bytes 6291460
  29.2 35.9 %all-to-all-start = ((bf16[128,4,2048]{2,1,0:T(4,128)(2,1)}), bf16[128,4,2048]{2,1,0:T(4,128)(2,1)}, u32[]{:S(2)}, u32[]{:S(2)}) async-start(bf16[128,4,2048]{2,1,0:T(4,128)(2,1)} %reshape.163), calls=%async_computation | async-start | bytes 4194304 | tf_op jit(solution)/shard_map/all_to_all | solution.py:458
  39.3 9.6 %copy-start.3 = (bf16[2048,128]{1,0:T(8,128)(2,1)S(1)}, bf16[2048,128]{1,0:T(8,128)(2,1)}, u32[]{:S(2)}) copy-start(bf16[2048,128]{1,0:T(8,128)(2,1)} %w_ref.1) | copy-start | bytes 1572868
  46.9 1.9 %copy-start.2 = (f32[512,2048]{1,0:T(8,128)}, f32[512,2048]{1,0:T(8,128)S(1)}, u32[]{:S(2)}) copy-start(f32[512,2048]{1,0:T(8,128)S(1)} %get-tuple-element.25.hid_any) | copy-start | bytes 12582916
  50.0 2.2 %copy-start.1 = (bf16[16384,128]{1,0:T(8,128)(2,1)S(1)}, bf16[16384,128]{1,0:T(8,128)(2,1)}, u32[]{:S(2)}) copy-start(bf16[16384,128]{1,0:T(8,128)(2,1)} %bank_ref.1) | copy-start | bytes 12582916
  65.1 10.6 %copy-start.4 = (bf16[2048,128]{1,0:T(8,128)(2,1)S(1)}, bf16[2048,128]{1,0:T(8,128)(2,1)}, u32[]{:S(2)}) copy-start(bf16[2048,128]{1,0:T(8,128)(2,1)} %param.15) | copy-start | bytes 1572868
  77.4 17.5 %all-to-all-start.1 = ((f32[128,4,128]{2,1,0:T(4,128)}), f32[128,4,128]{2,1,0:T(4,128)S(1)}, u32[]{:S(2)}, u32[]{:S(2)}) async-start(f32[128,4,128]{2,1,0:T(4,128)} %copy.24), calls=%async_computation.1 | async-start | bytes 524288 | tf_op jit(solution)/shard_map/all_to_all | solution.py:466
